TPU v7x, 32 devices: a whole 2x2x4 slice. The times are simulated.
32 devices in a mesh: gx: 16 (over z, y, core), gy: 2 (over x).
Axes of the slice: x: 2, y: 2, z: 4, core: 2. Of those that a mesh axis runs over, the one named last changes fastest.
Arguments:
- charge: float32 [512, 2048], P('gx', 'gy'), may hold values from -8 to 8
Outputs:
- potential: float32 [512, 2048], P('gx', 'gy')
All inputs are finite; a program needn't handle non-finite values.
Results may differ from a plain program's by a relative error of at most 0.0003.
Values sent between devices are 32-bit elements; how exact they have to be, the bound alone decides.
A program may use at most 128 MiB of HBM per device.

v0:
```python
import functools

import jax
import jax.numpy as jnp
import ml_dtypes
import numpy as np
from jax import lax
from jax.experimental import pallas as pl
from jax.experimental.pallas import tpu as pltpu
from jax.sharding import PartitionSpec as P

P_SIZE = 32
W = 16
Q = 4
NL = 16
CLASSES = [(0, 0), (0, 1), (1, 0), (1, 1)]
MESH = pl.DeviceIdType.MESH


def sine_table(length):
    counter = np.arange(length) + 1
    return np.sin(np.pi * np.outer(counter, counter) / (length + 1))


def eigen_values(length):
    return 2.0 - 2.0 * np.cos(np.pi * (np.arange(length) + 1) / (length + 1))


def interp_table(fine_start, fine_count, coarse_start, coarse_count, ratio):
    fine_pos = np.arange(fine_count) + fine_start
    coarse_pos = np.arange(coarse_count) + coarse_start
    numerator = 2 * fine_pos - (ratio - 1)
    lower = numerator // (2 * ratio)
    weight = ((numerator - 2 * ratio * lower) / (2 * ratio))[:, None]
    below = coarse_pos[None, :] == lower[:, None]
    above = coarse_pos[None, :] == lower[:, None] + 1
    return below * (1.0 - weight) + above * weight


def legendre_basis(length, count):
    points = (2.0 * np.arange(length) + 1.0) / length - 1.0
    columns = [np.ones_like(points), points]
    for degree in range(2, count):
        columns.append(
            ((2 * degree - 1) * points * columns[-1] - (degree - 1) * columns[-2]) / degree
        )
    result = []
    for vector in columns[:count]:
        for passes in range(2):
            for earlier in result:
                vector = vector - np.sum(earlier * vector) * earlier
        result.append(vector / np.sqrt(np.sum(vector * vector)))
    return np.stack(result, axis=1)


def fold(length):
    half = length // 2
    eye = np.eye(length)
    return np.concatenate([eye[:half] + eye[::-1][:half], eye[:half] - eye[::-1][:half]])


def split(table):
    high = table.astype(ml_dtypes.bfloat16)
    low = (table - high.astype(np.float64)).astype(ml_dtypes.bfloat16)
    return high, low


def pack(blocks):
    parts, places, row = [], {}, 0
    for name, block in blocks.items():
        rows = -(-block.shape[0] // 16) * 16
        part = np.zeros((rows, 128), np.float32)
        part[: block.shape[0], : block.shape[1]] = block
        parts.append(part)
        places[name] = (row, rows, block.shape[1])
        row += rows
    return np.concatenate(parts), places


@functools.lru_cache(maxsize=None)
def tables(n_gx, n_gy):
    n, length, cells = P_SIZE, P_SIZE + 2 * W, P_SIZE // Q
    blocks, margin = length // Q, W // Q
    half, hl, hb, hn = n // 2, length // 2, blocks // 2, NL // 2
    nx, ny, nz = n_gx * cells, n_gy * cells, cells
    modes = ny * nz
    s_l, s_n = sine_table(length), sine_table(n)
    u_n, u_b = fold(n), fold(blocks)
    basis = legendre_basis(n, NL)
    average = np.kron(np.eye(blocks), np.full((1, Q), 1.0 / Q))
    fine = interp_table(0, length, 0, blocks, Q)
    middle = fine[W : W + n]
    picks = [W - 1, W, W + n - 1, W + n]

    big = {}
    big["fold"] = np.concatenate(
        [np.kron(u_n[p * half : (p + 1) * half], u_n[q * half : (q + 1) * half]) for p, q in CLASSES]
    ).T
    inner = s_l[:, W : W + n] @ u_n.T / 2
    f1 = [inner[p::2, p * half : (p + 1) * half] for p in (0, 1)]
    big["fwd"] = np.stack([np.kron(f1[p], f1[q]).T for p, q in CLASSES])
    a_full = average @ s_l
    b_full = basis.T @ s_l[W : W + n]
    a1 = [(u_b @ a_full)[p * hb : (p + 1) * hb, p::2] for p in (0, 1)]
    b1 = [b_full[p::2, p::2] for p in (0, 1)]
    back = []
    for p, q in CLASSES:
        part = np.zeros((hl * hl, 256))
        part[:, 0:64] = np.kron(a1[p], a1[q]).T
        part[:, 64:128] = np.kron(b1[p], b1[q]).T
        part[:, 128:192] = np.kron(s_l[picks][:, p::2], b_full[:, q::2]).T
        back.append(part)
    big["back"] = np.stack(back)

    unfold = u_b.T / 2
    pair = np.kron(unfold, unfold).reshape(blocks * blocks, 2, hb, 2, hb)

    def from_samples(table):
        folded = np.einsum("os,spaqb->pqabo", table, pair)
        out = np.zeros((4, 128, table.shape[0]))
        for c, (p, q) in enumerate(CLASSES):
            out[c, :64] = folded[p, q].reshape(hb * hb, -1)
        return out.reshape(512, -1)

    bm = basis.T @ middle
    lin_x = from_samples(np.kron(bm, bm)).reshape(512, NL, NL)
    lin = np.zeros((512, 640))
    for c, (p, q) in enumerate(CLASSES):
        lin[:, c * 128 + 64 : c * 128 + 128] = lin_x[:, p::2, q::2].reshape(512, hn * hn)
    lin[:, 512:576] = from_samples(np.kron(fine[picks], bm))
    big["lin"] = lin
    k1 = [(s_n @ u_n.T / 2)[p::2, p * half : (p + 1) * half] for p in (0, 1)]
    big["near"] = np.stack([np.kron(k1[p], k1[q]).T for p, q in CLASSES])
    r1 = [(u_n @ s_n / 2)[p * half : (p + 1) * half, p::2] for p in (0, 1)]
    big["far"] = np.stack([np.kron(r1[p], r1[q]).T for p, q in CLASSES])

    second = 2 * np.eye(blocks) - np.eye(blocks, k=1) - np.eye(blocks, k=-1)
    s_y, s_z = sine_table(ny), sine_table(nz)
    proj_z = np.zeros((nz, blocks))
    proj_z[:, margin : margin + cells] = s_z
    spread, drop = [], []
    edge = interp_table(-1, n + 2, -1, cells + 2, Q)
    depth = interp_table(0, n, 0, cells, Q)
    lateral = edge[1 : n + 1]
    s_ext = np.zeros((ny + 2, ny))
    s_ext[1:-1] = s_y
    sp = np.concatenate([s_n[0::2], s_n[1::2]])
    deep = sp @ depth @ s_z

    def by_class(first, second_table):
        parts = []
        for p, q in CLASSES:
            parts.append(
                np.kron(first[p * half : (p + 1) * half], second_table[q * half : (q + 1) * half])
            )
        return np.concatenate(parts).T

    factor = (2.0 / (ny + 1)) * (2.0 / (nz + 1))
    for b in range(n_gy):
        proj_y = np.zeros((ny, blocks))
        for j in range(blocks):
            at = j + b * cells - margin
            if 0 <= at < ny:
                proj_y[:, j] = s_y[:, at]
        plain = np.kron(proj_y, proj_z)
        curved = np.kron(proj_y @ second, proj_z) + np.kron(proj_y, proj_z @ second)
        spread.append(
            factor * np.concatenate([from_samples(curved), from_samples(plain)])
        )
        local_s = s_ext[b * cells : b * cells + cells + 2]
        rim = np.outer(sp[:, 0], edge[0] @ local_s) + np.outer(sp[:, n - 1], edge[n + 1] @ local_s)
        drop.append(
            np.concatenate([by_class(sp @ lateral @ local_s, deep), by_class(rim, deep)])
        )
    big["spread"] = np.stack(spread)
    big["drop"] = np.stack(drop)
    sb = s_n @ basis
    sbp = np.concatenate([sb[0::2], sb[1::2]])
    wcx = np.zeros((512, n * n))
    for c, (p, q) in enumerate(CLASSES):
        wcx[c * 128 + 64 : c * 128 + 128, c * 256 : c * 256 + 256] = np.kron(
            sb[p::2, p::2], sb[q::2, q::2]
        ).T
    big["facex"] = wcx
    ends = np.stack([sp[:, 0], sp[:, n - 1], sp[:, 0], sp[:, n - 1]], axis=1)
    wcy = np.zeros((128, n * n))
    wcy[:64] = by_class(ends, sbp)
    big["facey"] = wcy

    mu_y, mu_z = eigen_values(ny), eigen_values(nz)
    theta = np.arccosh(1.0 + (mu_y[:, None] + mu_z[None, :]).reshape(1, modes) / 2)
    below = 2 * np.sinh(theta) * (1.0 - np.exp(-2 * theta * (nx + 1)))
    rows = 2 * nx + 16
    apart = np.abs(np.arange(rows) - nx)[:, None]
    toep = (np.exp(-theta * apart) + np.exp(-theta * np.maximum(2 * (nx + 1) - apart, 0))) / below
    total = (np.arange(rows) - 1)[:, None]
    hank = (np.exp(-theta * (total + 2)) + np.exp(-theta * np.maximum(2 * nx - total, 0))) / below
    green = np.stack([toep, hank]).astype(np.float32)
    green = green.reshape(2, rows, modes // 128, 128).transpose(0, 2, 1, 3)

    mu_l, mu_n = eigen_values(length), eigen_values(n)
    sums = np.ones((8, 4 * hl * hl), np.float32)
    sums[0] = np.concatenate(
        [(mu_l[p::2][:, None] + mu_l[q::2][None, :]).ravel() for p, q in CLASSES]
    )
    sums[1, : n * n] = np.concatenate(
        [(mu_n[p::2][:, None] + mu_n[q::2][None, :]).ravel() for p, q in CLASSES]
    )
    left = np.zeros((48, length))
    left[:16] = a_full
    left[16:20] = s_l[picks]
    left[32:48] = b_full
    flat = np.zeros((32, blocks))
    flat[:4] = fine[picks]
    flat[16:32] = bm
    u12 = np.zeros((64, 16))
    u12[:32, :10] = np.outer(s_n[:, 0], edge[0]) + np.outer(s_n[:, n - 1], edge[n + 1])
    u12[32:, :10] = s_n @ lateral
    lf = np.zeros((32, 24))
    lf[:, 0], lf[:, 3] = s_n[:, 0], s_n[:, n - 1]
    lf[:, 8 + 2] = s_n[:, 0]
    lf[:, 16 + 1] = s_n[:, n - 1]
    small, places = pack(
        {
            "sl": s_l[:, W : W + n],
            "left": left * (2.0 / (length + 1)) ** 3,
            "flat": flat,
            "second": second,
            "sn": s_n,
            "u12": u12,
            "lf": lf,
            "sb": sb,
            "mul": mu_l[:, None],
            "mun": mu_n[:, None],
        }
    )
    return big, green, sums, small, places


def halves(value):
    high = value.astype(jnp.bfloat16)
    return high, (value - high.astype(jnp.float32)).astype(jnp.bfloat16)


def mm(left, right):
    return jnp.dot(left, right, preferred_element_type=jnp.float32)


def right_mul(value, table):
    rows = value.shape[0]
    high, low = halves(value)
    both = mm(jnp.concatenate([high, low], axis=0), table[0])
    return both[:rows] + both[rows:] + mm(high, table[1])


def left_mul(table, value):
    rows = table.shape[0]
    th, tl = halves(table)
    vh, vl = halves(value)
    both = mm(jnp.concatenate([th, tl], axis=0), vh)
    return both[:rows] + both[rows:] + mm(th, vl)


NAMES = ["fold", "fwd", "back", "lin", "spread", "near", "facex", "facey", "drop", "far"]


def kernel(names, places, n_gx, n_gy, *refs):
    count = len(names)
    charge_ref, small_ref, sums_ref = refs[:3]
    hbm = dict(zip(names, refs[3 : 3 + count]))
    out_ref = refs[3 + count]
    vmem = dict(zip(names, refs[4 + count : 4 + 2 * count]))
    (pack_ref, cx_ref, cy_ref, all_ref, rx_ref, ry_ref, src_ref, load_sem, s_sem, r_sem, n_send, n_recv) = refs[
        4 + 2 * count :
    ]
    ndev = n_gx * n_gy
    a = lax.axis_index("gx")
    b = lax.axis_index("gy")
    me = a * n_gy + b
    n, cells = P_SIZE, P_SIZE // Q

    loads = {}
    for i, name in enumerate(names):
        source = hbm[name]
        if name[:-1] in ("spread", "drop"):
            source = source.at[b]
        loads[name] = pltpu.make_async_copy(source, vmem[name], load_sem.at[i])
        loads[name].start()

    barrier = pltpu.get_barrier_semaphore()

    def greet(r, carry):
        peer = lax.rem(me + r, ndev)
        pl.semaphore_signal(
            barrier, inc=1, device_id=(peer // n_gy, lax.rem(peer, n_gy)), device_id_type=MESH
        )
        return carry

    lax.fori_loop(1, ndev, greet, 0)

    def small(name):
        row, rows, cols = places[name]
        return small_ref[row : row + rows, 0:cols]

    def table(name, index=None):
        if index is None:
            return vmem[name + "0"][...], vmem[name + "1"][...]
        return vmem[name + "0"][index], vmem[name + "1"][index]

    def ready(*wanted):
        for name in wanted:
            loads[name].wait()

    charge = charge_ref[...]
    ready("fold0")
    folding = vmem["fold0"][...]
    high, low = halves(charge)
    both = mm(jnp.concatenate([high, low], axis=0), folding)
    folded = both[:n] + both[n:]
    wide = left_mul(small("sl"), folded)
    ready("fwd0", "fwd1", "back0", "back1")
    samples, cx = [], []
    cy = None
    for c in range(4):
        spectrum = right_mul(wide[:, c * 256 : (c + 1) * 256], table("fwd", c))
        spectrum = spectrum / (small("mul") + sums_ref[0:1, c * 1024 : (c + 1) * 1024])
        out = right_mul(left_mul(small("left"), spectrum), table("back", c))
        samples.append(out[0:16, 0:128])
        cx.append(out[16:32, 0:128])
        cy = out[32:48, 128:256] if cy is None else cy + out[32:48, 128:256]
    samples = jnp.concatenate(samples, axis=1)
    cx = jnp.concatenate(cx, axis=1)
    ready("spread0", "spread1")
    bent = left_mul(small("second"), samples)
    packet = right_mul(jnp.concatenate([samples, bent], axis=1), table("spread"))
    pack_ref[...] = packet

    pl.semaphore_wait(barrier, ndev - 1)

    def send(r):
        peer = lax.rem(me + r, ndev)
        return pltpu.make_async_remote_copy(
            src_ref=pack_ref,
            dst_ref=all_ref.at[me],
            send_sem=s_sem.at[r],
            recv_sem=r_sem.at[me],
            device_id=(peer // n_gy, lax.rem(peer, n_gy)),
            device_id_type=MESH,
        )

    def start(r, carry):
        send(r).start()
        return carry

    lax.fori_loop(1, ndev, start, 0)
    all_ref[me] = packet

    ready("lin0", "lin1")
    flat = right_mul(left_mul(small("flat"), samples), table("lin"))
    cx = cx - flat[0:16, 0:512]
    cy = cy - flat[16:32, 512:640]
    cx_ref[...] = cx[0:8]
    cy_ref[...] = cy
    right, left = lax.rem(a + 1, n_gx), lax.rem(a + n_gx - 1, n_gx)
    upper, lower = lax.rem(b + 1, n_gy), lax.rem(b + n_gy - 1, n_gy)
    near = []
    for i, (source, target, device) in enumerate(
        [
            (cx_ref, rx_ref.at[0], (right, b)),
            (cx_ref, rx_ref.at[1], (left, b)),
            (cy_ref, ry_ref.at[0], (a, upper)),
            (cy_ref, ry_ref.at[1], (a, lower)),
        ]
    ):
        copy = pltpu.make_async_remote_copy(
            src_ref=source,
            dst_ref=target,
            send_sem=n_send.at[i],
            recv_sem=n_recv.at[i],
            device_id=device,
            device_id_type=MESH,
        )
        copy.start()
        near.append(copy)

    ready("near0", "near1", "facex0", "facex1", "facey0", "facey1")
    narrow = left_mul(small("sn"), folded)
    spectrum = jnp.concatenate(
        [right_mul(narrow[:, c * 256 : (c + 1) * 256], table("near", c)) for c in range(4)], axis=1
    )

    for copy in near:
        copy.wait()
    from_left = jnp.where(a > 0, rx_ref[0], 0.0)
    from_right = jnp.where(a < n_gx - 1, rx_ref[1], 0.0)
    faces = jnp.concatenate([cx[0:8], from_left, from_right], axis=0)
    spectrum = spectrum + right_mul(left_mul(small("lf"), faces), table("facex"))
    group = lax.broadcasted_iota(jnp.int32, (16, 128), 1) // 16
    total = jnp.where((group == 0) | (group == 3), cy, 0.0)
    total = total + jnp.where((group == 2) & (b > 0), ry_ref[0], 0.0)
    total = total + jnp.where((group == 1) & (b < n_gy - 1), ry_ref[1], 0.0)
    spectrum = spectrum + right_mul(left_mul(small("sb"), total), table("facey"))

    def arrive(r, carry):
        origin = lax.rem(me + ndev - r, ndev)
        pltpu.make_async_remote_copy(
            src_ref=pack_ref,
            dst_ref=all_ref.at[origin],
            send_sem=s_sem.at[r],
            recv_sem=r_sem.at[origin],
            device_id=(origin // n_gy, lax.rem(origin, n_gy)),
            device_id_type=MESH,
        ).wait()
        return carry

    lax.fori_loop(1, ndev, arrive, 0)

    src_ref[...] = jnp.zeros_like(src_ref)

    def gather(k, carry):
        part = all_ref[k * n_gy]
        for j in range(1, n_gy):
            part = part + all_ref[k * n_gy + j]
        place = pl.ds(pl.multiple_of(k * cells, cells), 16)
        src_ref[place] = src_ref[place] + part
        return carry

    lax.fori_loop(0, n_gx, gather, 0)
    nx = n_gx * cells
    source = src_ref[4 : 4 + nx]
    ready("toep", "hank")
    values = []
    for i in range(cells + 2):
        row = []
        for g in range(source.shape[1] // 128):
            influence = (
                vmem["toep"][g, pl.ds(nx + 1 - i - a * cells, nx)]
                - vmem["hank"][g, pl.ds(a * cells + i, nx)]
            )
            part = influence * source[:, g * 128 : (g + 1) * 128]
            row.append(jnp.sum(part, axis=0, keepdims=True))
        values.append(jnp.concatenate(row, axis=1))
    values.append(jnp.zeros((16 - len(values), source.shape[1]), jnp.float32))
    coarse = jnp.concatenate(values, axis=0)
    ready("drop0", "drop1", "far0", "far1")
    lifted = left_mul(small("u12"), coarse)
    spectrum = spectrum + right_mul(
        jnp.concatenate([lifted[:n], lifted[n:]], axis=1), table("drop")
    )
    spectrum = spectrum * ((2.0 / (n + 1)) ** 3) / (small("mun") + sums_ref[1:2, 0 : n * n])
    spectrum = left_mul(small("sn"), spectrum)
    final = jnp.concatenate(
        [right_mul(spectrum[:, c * 256 : (c + 1) * 256], table("far", c)) for c in range(4)], axis=1
    )
    high, low = halves(final)
    both = lax.dot_general(
        jnp.concatenate([high, low], axis=0),
        folding,
        (((1,), (1,)), ((), ())),
        preferred_element_type=jnp.float32,
    )
    out_ref[...] = both[:n] + both[n:]


def body(n_gx, n_gy, charge):
    big, green, sums, small, places = tables(n_gx, n_gy)
    names, arrays = [], []
    for name in NAMES:
        if name == "fold":
            names.append("fold0")
            arrays.append(big[name].astype(ml_dtypes.bfloat16))
            continue
        for i, part in enumerate(split(big[name])):
            names.append(name + str(i))
            arrays.append(part)
    names += ["toep", "hank"]
    arrays += [green[0], green[1]]
    scratch = []
    for name, array in zip(names, arrays):
        shape = array.shape[1:] if name[:-1] in ("spread", "drop") else array.shape
        scratch.append(pltpu.VMEM(shape, array.dtype))
    ndev = n_gx * n_gy
    cells = P_SIZE // Q
    modes = n_gy * cells * cells
    scratch += [
        pltpu.VMEM((16, modes), jnp.float32),
        pltpu.VMEM((8, 512), jnp.float32),
        pltpu.VMEM((16, 128), jnp.float32),
        pltpu.VMEM((ndev, 16, modes), jnp.float32),
        pltpu.VMEM((2, 8, 512), jnp.float32),
        pltpu.VMEM((2, 16, 128), jnp.float32),
        pltpu.VMEM((n_gx * cells + 8, modes), jnp.float32),
        pltpu.SemaphoreType.DMA((len(names),)),
        pltpu.SemaphoreType.DMA((ndev,)),
        pltpu.SemaphoreType.DMA((ndev,)),
        pltpu.SemaphoreType.DMA((4,)),
        pltpu.SemaphoreType.DMA((4,)),
    ]
    vm = pl.BlockSpec(memory_space=pltpu.VMEM)
    return pl.pallas_call(
        functools.partial(kernel, names, places, n_gx, n_gy),
        out_shape=jax.ShapeDtypeStruct(charge.shape, charge.dtype),
        in_specs=[vm] * 3 + [pl.BlockSpec(memory_space=pl.ANY)] * len(names),
        out_specs=vm,
        scratch_shapes=scratch,
        name="mlc",
        compiler_params=pltpu.CompilerParams(
            collective_id=0, has_side_effects=True, vmem_limit_bytes=60 * 1024 * 1024
        ),
    )(charge, small, sums, *[jnp.asarray(array) for array in arrays])


def solution(mesh):
    run = functools.partial(body, mesh.shape["gx"], mesh.shape["gy"])
    spec = P("gx", "gy")
    return jax.shard_map(run, mesh=mesh, in_specs=(spec,), out_specs=spec, check_vma=False)
```

profile of v0, /device:TPU:0, one launch (start us, length us, event | category | flops | bytes accessed | tf_op | source)
XLA Modules:
  0.0 23.9 jit_solution(15491096071201946859)
XLA Ops:
  0.0 22.3 %mlc.1 = f32[32,1024]{1,0:T(8,128)} custom-call(f32[32,1024]{1,0:T(8,128)} %refs_0_.1, f32[416,128]{1,0:T(8,128)} %constant.67.clone.refs_1_, f32[8,4096]{1,0:T(8,128)} %constant.68.clone.refs_2_, bf16[1024,1024]{1,0:T(8,128)(2,1)} %constant.46.clone.refs_3_, bf16[4,256,1024]{2,1,0:T(8,128)(2,1)} %constant.47.clone.refs_4_, ...), custom_call_target="tpu_custom_call" | custom-call | tf_op jit(solution)/shard_map/mlc/pallas_call | solution.py:500
  22.4 1.6 %copy.26 = f32[32,1024]{1,0:T(8,128)} copy(f32[32,1024]{1,0:T(8,128)} %mlc.1) | data formatting | bytes 262144
where the time goes:
time: 24.1 us; the launch traced here: 23.9 us
  Pallas kernels  22.3 us (93%)
  local copies, waits for them, and re-layouts  1.57 us (7%)
    pallas_call x1, Pallas kernels, body(): pl.pallas_call(functools.partial(kernel, names, places, n_gx, n_gy), out_...  22.3 us
    unnamed x1, local copies, waits for them, and re-layouts  1.57 us

commit v1 on v0

v1 whole, which is shorter than its diff:
```python
import functools

import jax
import jax.numpy as jnp
import ml_dtypes
import numpy as np
from jax import lax
from jax.experimental import pallas as pl
from jax.experimental.pallas import tpu as pltpu
from jax.sharding import PartitionSpec as P

P_SIZE = 32
W = 16
Q = 4
NL = 16
CLASSES = [(0, 0), (0, 1), (1, 0), (1, 1)]
MESH = pl.DeviceIdType.MESH


def sine_table(length):
    counter = np.arange(length) + 1
    return np.sin(np.pi * np.outer(counter, counter) / (length + 1))


def eigen_values(length):
    return 2.0 - 2.0 * np.cos(np.pi * (np.arange(length) + 1) / (length + 1))


def interp_table(fine_start, fine_count, coarse_start, coarse_count, ratio):
    fine_pos = np.arange(fine_count) + fine_start
    coarse_pos = np.arange(coarse_count) + coarse_start
    numerator = 2 * fine_pos - (ratio - 1)
    lower = numerator // (2 * ratio)
    weight = ((numerator - 2 * ratio * lower) / (2 * ratio))[:, None]
    below = coarse_pos[None, :] == lower[:, None]
    above = coarse_pos[None, :] == lower[:, None] + 1
    return below * (1.0 - weight) + above * weight


def legendre_basis(length, count):
    points = (2.0 * np.arange(length) + 1.0) / length - 1.0
    columns = [np.ones_like(points), points]
    for degree in range(2, count):
        columns.append(
            ((2 * degree - 1) * points * columns[-1] - (degree - 1) * columns[-2]) / degree
        )
    result = []
    for vector in columns[:count]:
        for passes in range(2):
            for earlier in result:
                vector = vector - np.sum(earlier * vector) * earlier
        result.append(vector / np.sqrt(np.sum(vector * vector)))
    return np.stack(result, axis=1)


def fold(length):
    half = length // 2
    eye = np.eye(length)
    return np.concatenate([eye[:half] + eye[::-1][:half], eye[:half] - eye[::-1][:half]])


def split(table):
    high = table.astype(ml_dtypes.bfloat16)
    low = (table - high.astype(np.float64)).astype(ml_dtypes.bfloat16)
    return high, low


def pack(blocks, row_tile):
    parts, places, row = [], {}, 0
    for name, block in blocks.items():
        rows = -(-block.shape[0] // row_tile) * row_tile
        part = np.zeros((rows, 128))
        part[: block.shape[0], : block.shape[1]] = block
        parts.append(part)
        places[name] = (row, rows, block.shape[1])
        row += rows
    return np.concatenate(parts), places


@functools.lru_cache(maxsize=None)
def tables(n_gx, n_gy):
    n, length, cells = P_SIZE, P_SIZE + 2 * W, P_SIZE // Q
    blocks, margin = length // Q, W // Q
    half, hl, hb, hn = n // 2, length // 2, blocks // 2, NL // 2
    quad, wide = hb * hb, hn * hn
    nx, ny, nz = n_gx * cells, n_gy * cells, cells
    modes = ny * nz
    s_l, s_n = sine_table(length), sine_table(n)
    u_n, u_b = fold(n), fold(blocks)
    basis = legendre_basis(n, NL)
    average = np.kron(np.eye(blocks), np.full((1, Q), 1.0 / Q))
    fine = interp_table(0, length, 0, blocks, Q)
    middle = fine[W : W + n]
    picks = [W - 1, W, W + n - 1, W + n]
    a_full = average @ s_l
    b_full = basis.T @ s_l[W : W + n]
    swapped = [1, 0, 3, 2]
    big = {}

    folding = np.zeros((4, 4, n, 4, 2 * 4, half))
    for c, (p, q) in enumerate(CLASSES):
        for vi in range(4):
            for y4 in range(4):
                il = [y4, 4 + y4, 3 - y4, 7 - y4][vi]
                sign = -1.0 if vi > 1 and p == 1 else 1.0
                folding[vi, y4, :, c, il, :] = sign * u_n[q * half : (q + 1) * half].T
    folding = folding.reshape(4 * 128, 4 * 128)
    plain = {"fold": folding, "unfold": folding.T}

    inner = s_l[:, W : W + n] @ u_n.T / 2
    f1 = [inner[p::2, p * half : (p + 1) * half] for p in (0, 1)]
    a1 = [(u_b @ a_full)[p * hb : (p + 1) * hb, p::2] for p in (0, 1)]
    b1 = [b_full[p::2, p::2] for p in (0, 1)]
    for c, (p, q) in enumerate(CLASSES):
        big["fwd%d" % c] = np.kron(f1[p], f1[q]).T
        part = np.zeros((hl * hl, 256))
        sample, coef = np.kron(a1[p], a1[q]).T, np.kron(b1[p], b1[q]).T
        part[:, :128] = np.concatenate([sample, coef] if c % 2 == 0 else [coef, sample], axis=1)
        part[:, 128:192] = np.kron(s_l[picks][:, p::2], b_full[:, q::2]).T
        big["back%d" % c] = part

    unfold = u_b.T / 2
    pair = np.kron(unfold, unfold).reshape(blocks * blocks, 2, hb, 2, hb)

    def from_samples(table):
        folded = np.einsum("os,spaqb->pqabo", table, pair)
        return folded.reshape(4 * quad, table.shape[0])

    bm = basis.T @ middle
    lin_x = from_samples(np.kron(bm, bm)).reshape(4 * quad, NL, NL)
    lin = np.zeros((4 * quad, 384))
    for place, c in enumerate(swapped):
        p, q = CLASSES[c]
        lin[:, place * wide : (place + 1) * wide] = lin_x[:, p::2, q::2].reshape(4 * quad, wide)
    lin[:, 256:320] = from_samples(np.kron(fine[picks], bm))
    big["lin"] = lin
    k1 = [(s_n @ u_n.T / 2)[p::2, p * half : (p + 1) * half] for p in (0, 1)]
    big["near"] = np.concatenate([np.kron(k1[p], k1[q]).T for p, q in CLASSES])
    r1 = [(u_n @ s_n / 2)[p * half : (p + 1) * half, p::2] for p in (0, 1)]
    big["far"] = np.concatenate([np.kron(r1[p], r1[q]).T for p, q in CLASSES])

    second = 2 * np.eye(blocks) - np.eye(blocks, k=1) - np.eye(blocks, k=-1)
    s_y, s_z = sine_table(ny), sine_table(nz)
    proj_z = np.zeros((nz, blocks))
    proj_z[:, margin : margin + cells] = s_z
    edge = interp_table(-1, n + 2, -1, cells + 2, Q)
    depth = interp_table(0, n, 0, cells, Q)
    lateral = edge[1 : n + 1]
    s_ext = np.zeros((ny + 2, ny))
    s_ext[1:-1] = s_y
    sp = np.concatenate([s_n[0::2], s_n[1::2]])
    deep = sp @ depth @ s_z

    def by_class(first, second_table):
        parts = []
        for p, q in CLASSES:
            parts.append(
                np.kron(first[p * half : (p + 1) * half], second_table[q * half : (q + 1) * half])
            )
        return np.concatenate(parts).T

    factor = (2.0 / (ny + 1)) * (2.0 / (nz + 1))
    spread, drop = [], []
    for b in range(n_gy):
        proj_y = np.zeros((ny, blocks))
        for j in range(blocks):
            at = j + b * cells - margin
            if 0 <= at < ny:
                proj_y[:, j] = s_y[:, at]
        flat = np.kron(proj_y, proj_z)
        curved = np.kron(proj_y @ second, proj_z) + np.kron(proj_y, proj_z @ second)
        spread.append(
            factor * np.concatenate([from_samples(curved), from_samples(flat)], axis=1)
        )
        local_s = s_ext[b * cells : b * cells + cells + 2]
        rim = np.outer(sp[:, 0], edge[0] @ local_s) + np.outer(sp[:, n - 1], edge[n + 1] @ local_s)
        drop.append(
            np.concatenate([by_class(sp @ lateral @ local_s, deep), by_class(rim, deep)])
        )
    big["spread"] = np.stack(spread)
    big["drop"] = np.stack(drop)
    sb = s_n @ basis
    sbp = np.concatenate([sb[0::2], sb[1::2]])
    facex = np.zeros((4 * wide, n * n))
    for place, c in enumerate(swapped):
        p, q = CLASSES[c]
        facex[place * wide : (place + 1) * wide, c * 256 : c * 256 + 256] = np.kron(
            sb[p::2, p::2], sb[q::2, q::2]
        ).T
    big["facex"] = facex
    ends = np.stack([sp[:, 0], sp[:, n - 1], sp[:, 0], sp[:, n - 1]], axis=1)
    big["facey"] = by_class(ends, sbp)

    mu_y, mu_z = eigen_values(ny), eigen_values(nz)
    theta = np.arccosh(1.0 + (mu_y[:, None] + mu_z[None, :]).reshape(1, modes) / 2)
    below = 2 * np.sinh(theta) * (1.0 - np.exp(-2 * theta * (nx + 1)))
    apart = np.abs(np.arange(48) - 20)[:, None]
    toep = (np.exp(-theta * apart) + np.exp(-theta * np.maximum(2 * (nx + 1) - apart, 0))) / below
    total = (np.arange(2 * nx + 32) - 13)[:, None]
    hank = np.exp(-theta * np.maximum(total + 2, 0)) + np.exp(-theta * np.maximum(2 * nx - total, 0))
    hank = hank / below

    u12 = np.zeros((64, 16))
    u12[:32, :10] = np.outer(s_n[:, 0], edge[0]) + np.outer(s_n[:, n - 1], edge[n + 1])
    u12[32:, :10] = s_n @ lateral
    place = np.arange(n_gx)
    mine = []
    for a in range(n_gx):
        rank = np.arange(16)[:, None]
        at = cells * a - margin + rank
        inside = (at >= 0) & (at < nx)
        rightward = inside * np.exp(-theta * (15 - rank)) * (1 - np.exp(-2 * theta * (at + 1) * inside))
        leftward = inside * np.exp(-theta * rank) * (1 - np.exp(-2 * theta * (nx - at) * inside))
        row = np.arange(16)[:, None]
        x = cells * a - 1 + row
        used = row < cells + 2
        falling = used * np.exp(-theta * row) * (1 - np.exp(-2 * theta * np.maximum(nx - x, 0))) / below
        rising = (
            used
            * np.exp(-theta * np.maximum(cells + 1 - row, 0))
            * (1 - np.exp(-2 * theta * (x + 1)))
            / below
        )
        away = (a - place)[:, None]
        before = (away >= 2) * np.exp(-theta * np.maximum(cells * away - 12, 0))
        after = (away <= -2) * np.exp(-theta * np.maximum(-cells * away - 12, 0))
        mine.append(
            np.concatenate([rightward, leftward, u12 @ falling, u12 @ rising, before, after])
        )
    singles = {
        "mine": np.stack(mine).astype(np.float32),
        "toep": toep.astype(np.float32),
        "hank": hank.astype(np.float32),
    }

    mu_l, mu_n = eigen_values(length), eigen_values(n)
    sums = np.ones((8, hl * hl))
    for c, (p, q) in enumerate(CLASSES):
        sums[c] = (mu_l[p::2][:, None] + mu_l[q::2][None, :]).ravel()
    sums[4, : n * n] = np.concatenate(
        [(mu_n[p::2][:, None] + mu_n[q::2][None, :]).ravel() for p, q in CLASSES]
    )
    singles["sums"] = sums.astype(np.float32)
    columns, column_places = pack(
        {"mul": mu_l[:, None], "mun": mu_n[:, None], "ends": s_n[:, [0, n - 1]]}, 8
    )
    singles["columns"] = columns.astype(np.float32)

    scale = (2.0 / (length + 1)) ** 3
    flat = np.zeros((24, length))
    flat[:4] = fine[picks] @ a_full * scale
    flat[8:24] = bm @ a_full * scale
    lefts = {
        "sl": s_l[:, W : W + n],
        "source": np.concatenate([a_full, second @ a_full], axis=1) * scale,
        "flat": flat,
        "picks": s_l[picks] * scale,
        "coefs": b_full * scale,
        "sn": s_n,
        "u12": u12,
        "sb": sb,
    }
    left, left_places = pack(lefts, 16)
    doubled, row, spots = [], 0, {}
    for name, (start, rows, cols) in left_places.items():
        doubled += list(split(left[start : start + rows]))
        spots[name] = (row, rows, cols)
        row += 2 * rows
    singles["lefts"] = np.concatenate(doubled)
    for name, value in plain.items():
        singles[name] = value.astype(ml_dtypes.bfloat16)
    for name, value in big.items():
        singles[name] = np.stack(split(value), axis=value.ndim - 2)
    return singles, column_places, spots


def halves(value):
    high = value.astype(jnp.bfloat16)
    return high, (value - high.astype(jnp.float32)).astype(jnp.bfloat16)


def mm(left, right):
    return jnp.dot(left, right, preferred_element_type=jnp.float32)


def right_mul(value, high_table, low_table):
    rows = value.shape[0]
    high, low = halves(value)
    both = mm(jnp.concatenate([high, low], axis=0), high_table)
    return both[:rows] + both[rows:] + mm(high, low_table)


NAMES = [
    "charge", "fold", "lefts", "sums", "columns",
    "fwd0", "fwd1", "back0", "fwd2", "back1", "fwd3", "back2", "back3",
    "spread", "mine", "lin", "near", "facex", "facey", "toep", "hank", "drop", "far", "unfold",
]


def window(name, shape):
    if name in ("spread", "drop", "mine"):
        return shape[1:]
    if name == "hank":
        return (48,) + shape[1:]
    return shape


def kernel(column_places, spots, n_gx, n_gy, *refs):
    count = len(NAMES)
    hbm = dict(zip(NAMES, refs[:count]))
    out_ref = refs[count]
    vmem = dict(zip(NAMES, refs[count + 1 : 2 * count + 1]))
    (
        mom_ref, far_ref, near_ref, cx_ref, cy_ref, rx_ref, ry_ref,
        load_sem, f_send, f_recv, p_send, p_recv, c_send, c_recv,
    ) = refs[2 * count + 1 :]
    ndev = n_gx * n_gy
    a = lax.axis_index("gx")
    b = lax.axis_index("gy")
    me = a * n_gy + b
    n, cells = P_SIZE, P_SIZE // Q

    loads = {}
    for i, name in enumerate(NAMES):
        source = hbm[name]
        if name in ("spread", "drop"):
            source = source.at[b]
        if name == "mine":
            source = source.at[a]
        if name == "hank":
            source = source.at[pl.ds(pl.multiple_of(a * 16, 16), 48)]
        loads[name] = pltpu.make_async_copy(source, vmem[name], load_sem.at[i])
        loads[name].start()

    barrier = pltpu.get_barrier_semaphore()

    def greet(r, carry):
        peer = lax.rem(me + r, ndev)
        pl.semaphore_signal(
            barrier, inc=1, device_id=(peer // n_gy, lax.rem(peer, n_gy)), device_id_type=MESH
        )
        return carry

    with jax.named_scope("greet"):
        lax.fori_loop(1, ndev, greet, 0)

    def ready(*wanted):
        for name in wanted:
            loads[name].wait()

    def table(name):
        return vmem[name][0], vmem[name][1]

    def column(name):
        row, rows, cols = column_places[name]
        return vmem["columns"][row : row + rows, 0:cols]

    def left_mul(name, value):
        row, rows, cols = spots[name]
        high, low = halves(value)
        both = mm(vmem["lefts"][row : row + 2 * rows, 0:cols], high)
        rest = mm(vmem["lefts"][row : row + rows, 0:cols], low)
        return both[:rows] + both[rows:] + rest

    groups = [[0, 1, 7, 6], [2, 3, 5, 4]]
    with jax.named_scope("fold"):
        ready("charge", "fold")
        sides = [
            jnp.concatenate([vmem["charge"][:, v * 128 : (v + 1) * 128] for v in group], axis=1)
            for group in groups
        ]
        high, low = halves(jnp.concatenate(sides, axis=0))
        both = mm(jnp.concatenate([high, low], axis=0), vmem["fold"][...])
        both = both[: 2 * n] + both[2 * n :]
        folded = jnp.concatenate(
            [
                both[s * n : (s + 1) * n, c * 128 : (c + 1) * 128]
                for c in range(4)
                for s in range(2)
            ],
            axis=1,
        )
        ready("lefts")
        wide = left_mul("sl", folded)
        ready("sums", "columns")

    def forward(c):
        ready("fwd%d" % c)
        spectrum = right_mul(wide[:, c * 256 : (c + 1) * 256], *table("fwd%d" % c))
        return spectrum / (column("mul") + vmem["sums"][c : c + 1, :])

    def backward(c, spectrum):
        ready("back%d" % c)
        return right_mul(spectrum, *table("back%d" % c))

    with jax.named_scope("classes"):
        s0 = forward(0)
        s1 = forward(1)
        y0 = backward(0, s0)
        s2 = forward(2)
        y1 = backward(1, s1)
        s3 = forward(3)
        y2 = backward(2, s2)
        y3 = backward(3, s3)
    with jax.named_scope("spread"):
        first = lax.broadcasted_iota(jnp.int32, (n + 2 * W, 128), 1) < 64
        sample = jnp.concatenate(
            [jnp.where(first, u[:, :128], v[:, :128]) for u, v in ((y0, y1), (y2, y3))], axis=1
        )
        ready("spread", "mine")
        modes = near_ref.shape[-1]
        spread = right_mul(sample, *table("spread"))
        packet = left_mul("source", jnp.concatenate([spread[:, :modes], spread[:, modes:]], axis=0))
        near_ref[1, b] = packet
        mine = vmem["mine"]
        rightward = jnp.sum(packet * mine[0:16], axis=0, keepdims=True)
        leftward = jnp.sum(packet * mine[16:32], axis=0, keepdims=True)
        for g in range(modes // 128):
            mom_ref[g, 0:1] = rightward[:, g * 128 : (g + 1) * 128]
            mom_ref[g, 1:2] = leftward[:, g * 128 : (g + 1) * 128]

    with jax.named_scope("barrier"):
        pl.semaphore_wait(barrier, ndev - 1)

    def remote(source, target, send, recv, device):
        return pltpu.make_async_remote_copy(
            src_ref=source,
            dst_ref=target,
            send_sem=send,
            recv_sem=recv,
            device_id=device,
            device_id_type=MESH,
        )

    def start_far(r, carry):
        d = n_gx - r
        for j in range(n_gy):

            @pl.when(a + d < n_gx)
            def _():
                remote(
                    mom_ref.at[:, pl.ds(0, 1)],
                    far_ref.at[b, :, pl.ds(a, 1)],
                    f_send,
                    f_recv,
                    (a + d, j),
                ).start()

            @pl.when(a >= d)
            def _():
                remote(
                    mom_ref.at[:, pl.ds(1, 1)],
                    far_ref.at[b, :, pl.ds(a, 1)],
                    f_send,
                    f_recv,
                    (a - d, j),
                ).start()

        return carry

    def for_near(act):
        for step in (0, 1, 2):
            for j in range(n_gy):
                other = a + step - 1
                fine = (other >= 0) & (other < n_gx)
                if step == 1:
                    fine = b != j

                @pl.when(fine)
                def _():
                    act(step, j, (other, j))

    with jax.named_scope("send"):
        lax.fori_loop(1, n_gx - 1, start_far, 0)

        def send_near(step, j, device):
            remote(
                near_ref.at[1, b],
                near_ref.at[2 - step, b],
                p_send.at[step, j],
                p_recv.at[2 - step, b],
                device,
            ).start()

        for_near(send_near)

    with jax.named_scope("lin"):
        ready("lin")
        coef = jnp.concatenate(
            [jnp.where(first, v[:, :128], u[:, :128]) for u, v in ((y0, y1), (y2, y3))], axis=1
        )
        slab = y0[:, 128:] + y1[:, 128:] + y2[:, 128:] + y3[:, 128:]
        flat = right_mul(left_mul("flat", sample), *table("lin"))
        cx = left_mul("picks", coef)[0:8] - flat[0:8, 0:256]
        cy = left_mul("coefs", slab) - flat[8:24, 256:384]
        cx_ref[...] = cx
        cy_ref[...] = cy

    upper, lower = lax.rem(b + 1, n_gy), lax.rem(b + n_gy - 1, n_gy)
    go_right = remote(cx_ref.at[pl.ds(2, 1)], rx_ref.at[pl.ds(0, 1)], c_send.at[0], c_recv.at[0], (a + 1, b))
    go_left = remote(cx_ref.at[pl.ds(1, 1)], rx_ref.at[pl.ds(1, 1)], c_send.at[1], c_recv.at[1], (a - 1, b))
    go_up = remote(cy_ref, ry_ref.at[0], c_send.at[2], c_recv.at[2], (a, upper))
    go_down = remote(cy_ref, ry_ref.at[1], c_send.at[3], c_recv.at[3], (a, lower))

    with jax.named_scope("sendc"):

        @pl.when(a < n_gx - 1)
        def _():
            go_right.start()

        @pl.when(a > 0)
        def _():
            go_left.start()

        go_up.start()
        go_down.start()

    with jax.named_scope("near"):
        ready("near")
        narrow = left_mul("sn", folded)
        spectrum = jnp.concatenate(
            [
                right_mul(
                    narrow[:, c * 256 : (c + 1) * 256],
                    vmem["near"][0, c * 256 : (c + 1) * 256],
                    vmem["near"][1, c * 256 : (c + 1) * 256],
                )
                for c in range(4)
            ],
            axis=1,
        )
        scale = (2.0 / (n + 1)) ** 3
        inverse = scale / (column("mun") + vmem["sums"][4:5, 0 : n * n])

    with jax.named_scope("wait_c"):

        @pl.when(a < n_gx - 1)
        def _():
            go_right.wait_send()
            go_left.wait_recv()

        @pl.when(a > 0)
        def _():
            go_left.wait_send()
            go_right.wait_recv()

        go_up.wait()
        go_down.wait()

    with jax.named_scope("face"):
        ready("facex", "facey")
        from_left = jnp.where(a > 0, rx_ref[0:1], 0.0)
        from_right = jnp.where(a < n_gx - 1, rx_ref[1:2], 0.0)
        ends = jnp.concatenate(
            [cx[0:1] + from_left, cx[3:4] + from_right, jnp.zeros((6, cx.shape[1]), jnp.float32)]
        )
        ends = right_mul(ends, *table("facex"))
        spectrum = spectrum + column("ends")[:, 0:1] * ends[0:1]
        spectrum = spectrum + column("ends")[:, 1:2] * ends[1:2]
        group = lax.broadcasted_iota(jnp.int32, (16, 128), 1) // 16
        total = jnp.where((group == 0) | (group == 3), cy, 0.0)
        total = total + jnp.where((group == 2) & (b > 0), ry_ref[0], 0.0)
        total = total + jnp.where((group == 1) & (b < n_gy - 1), ry_ref[1], 0.0)
        spectrum = spectrum + right_mul(left_mul("sb", total)[:, 0:64], *table("facey"))

    with jax.named_scope("wait_p"):

        def wait_near(step, j, device):
            remote(
                near_ref.at[1, b], near_ref.at[step, j], p_send.at[step, j], p_recv.at[step, j], device
            ).wait()

        for_near(wait_near)

    with jax.named_scope("green"):
        ready("toep", "hank")
        row = lax.broadcasted_iota(jnp.int32, (8, modes), 0)

        def gathered(step):
            value = near_ref[step, 0]
            for j in range(1, n_gy):
                value = value + near_ref[step, j]
            return value

        past = jnp.where(a > 0, gathered(0), 0.0)
        here = gathered(1)
        next_ = jnp.where(a < n_gx - 1, gathered(2), 0.0)
        source = jnp.concatenate(
            [
                jnp.where((row >= 4) | (a > 1), past[0:8], 0.0),
                past[8:16] + jnp.where((row >= 4) | (a > 0), here[0:8], 0.0),
                jnp.where((row < 4) | (a < n_gx - 1), here[8:16] + next_[0:8], 0.0),
                jnp.where((row < 4) | (a < n_gx - 2), next_[8:16], 0.0),
            ]
        )
        values = []
        for i in range(cells + 2):
            influence = vmem["toep"][9 - i : 41 - i] - vmem["hank"][i : i + 32]
            values.append(jnp.sum(influence * source, axis=0, keepdims=True))
        values.append(jnp.zeros((16 - len(values), modes), jnp.float32))
        lifted = left_mul("u12", jnp.concatenate(values, axis=0))

    with jax.named_scope("wait_f"):

        def settle(each):
            block = far_ref.at[:, :, pl.ds(0, each)]
            remote(block, block, f_send, f_recv, (a, b)).wait()

        edge = (a == 0) | (a == n_gx - 1)

        @pl.when(edge)
        def _():
            settle(n_gx - 2)

        @pl.when(jnp.logical_not(edge))
        def _():
            settle(n_gx - 3)

    with jax.named_scope("final"):
        origin = lax.broadcasted_iota(jnp.int32, (n_gx, modes), 0)
        before = jnp.zeros((n_gx, modes), jnp.float32)
        after = before
        for j in range(n_gy):
            sent = jnp.concatenate([far_ref[j, g] for g in range(modes // 128)], axis=1)
            before = before + jnp.where(origin <= a - 2, sent, 0.0)
            after = after + jnp.where(origin >= a + 2, sent, 0.0)
        before = jnp.sum(before * mine[160 : 160 + n_gx], axis=0, keepdims=True)
        after = jnp.sum(after * mine[160 + n_gx : 160 + 2 * n_gx], axis=0, keepdims=True)
        lifted = lifted + mine[32:96] * before + mine[96:160] * after
        ready("drop", "far", "unfold")
        spectrum = spectrum + right_mul(
            jnp.concatenate([lifted[:n], lifted[n:]], axis=1), *table("drop")
        )
        spectrum = left_mul("sn", spectrum * inverse)
        parts = [
            right_mul(
                spectrum[:, c * 256 : (c + 1) * 256],
                vmem["far"][0, c * 256 : (c + 1) * 256],
                vmem["far"][1, c * 256 : (c + 1) * 256],
            )
            for c in range(4)
        ]
    with jax.named_scope("unfold"):
        sides = [
            jnp.concatenate([part[:, s * 128 : (s + 1) * 128] for part in parts], axis=1)
            for s in range(2)
        ]
        high, low = halves(jnp.concatenate(sides, axis=0))
        both = mm(jnp.concatenate([high, low], axis=0), vmem["unfold"][...])
        both = both[: 2 * n] + both[2 * n :]
        for s, group in enumerate(groups):
            for i, v in enumerate(group):
                out_ref[:, v * 128 : (v + 1) * 128] = both[
                    s * n : (s + 1) * n, i * 128 : (i + 1) * 128
                ]


def emit(in_ref, out_ref, sem):
    copy = pltpu.make_async_copy(in_ref, out_ref, sem)
    copy.start()
    copy.wait()


def body(n_gx, n_gy, charge):
    singles, column_places, spots = tables(n_gx, n_gy)
    arrays = [charge] + [jnp.asarray(singles[name]) for name in NAMES[1:]]
    scratch = [
        pltpu.VMEM(window(name, array.shape), array.dtype) for name, array in zip(NAMES, arrays)
    ]
    modes = n_gy * (P_SIZE // Q) ** 2
    scratch += [
        pltpu.VMEM((modes // 128, 8, 128), jnp.float32),
        pltpu.VMEM((n_gy, modes // 128, n_gx, 128), jnp.float32),
        pltpu.VMEM((3, n_gy, 16, modes), jnp.float32),
        pltpu.VMEM((8, 256), jnp.float32),
        pltpu.VMEM((16, 128), jnp.float32),
        pltpu.VMEM((8, 256), jnp.float32),
        pltpu.VMEM((2, 16, 128), jnp.float32),
        pltpu.SemaphoreType.DMA((len(NAMES),)),
        pltpu.SemaphoreType.DMA,
        pltpu.SemaphoreType.DMA,
        pltpu.SemaphoreType.DMA((3, n_gy)),
        pltpu.SemaphoreType.DMA((3, n_gy)),
        pltpu.SemaphoreType.DMA((4,)),
        pltpu.SemaphoreType.DMA((4,)),
    ]
    hbm = pl.BlockSpec(memory_space=pl.ANY)
    vm = pl.BlockSpec(memory_space=pltpu.VMEM)
    solved = pl.pallas_call(
        functools.partial(kernel, column_places, spots, n_gx, n_gy),
        out_shape=pltpu.VMEM(charge.shape, charge.dtype),
        in_specs=[hbm] * len(NAMES),
        out_specs=vm,
        scratch_shapes=scratch,
        name="mlc",
        compiler_params=pltpu.CompilerParams(
            collective_id=0, has_side_effects=True, vmem_limit_bytes=60 * 1024 * 1024
        ),
    )(*arrays)
    return pl.pallas_call(
        emit,
        out_shape=jax.ShapeDtypeStruct(charge.shape, charge.dtype),
        in_specs=[vm],
        out_specs=hbm,
        scratch_shapes=[pltpu.SemaphoreType.DMA],
        name="emit",
        compiler_params=pltpu.CompilerParams(vmem_limit_bytes=1024 * 1024),
    )(solved)


def solution(mesh):
    run = functools.partial(body, mesh.shape["gx"], mesh.shape["gy"])
    spec = P("gx", "gy")
    return jax.shard_map(run, mesh=mesh, in_specs=(spec,), out_specs=spec, check_vma=False)
```

time: 24.1 us -> 15.6 us (0.65)
  Pallas kernels: 22.3 us -> 15.5 us
  local copies, waits for them, and re-layouts: 1.57 us -> 0 us
    pallas_call x1 -> x2, Pallas kernels: 22.3 us -> 15.5 us  [the longest x1 14.8 us: body(): pl.pallas_call(functools.partial(kernel, column_places, spots, n_gx, n_gy...]
    unnamed x1 -> x0, local copies, waits for them, and re-layouts: 1.57 us -> none
where the time goes in v1:
time: 15.6 us; the launch traced here: 15.5 us
  Pallas kernels  15.5 us (99%)
    pallas_call x1, Pallas kernels, body(): pl.pallas_call(functools.partial(kernel, column_places, spots, n_gx, n_gy...  14.8 us
    pallas_call x1, Pallas kernels, body(): pl.pallas_call(emit, out_shape=jax.ShapeDtypeStruct(charge.shape, charge....  0.67 us

profile of v1, /device:TPU:0, one launch (start us, length us, event | category | flops | bytes accessed | tf_op | source)
XLA Modules:
  0.0 15.5 jit_solution(2423399096066770986)
XLA Ops:
  0.0 14.8 %mlc.1.in_ref = f32[32,1024]{1,0:T(8,128)S(1)} custom-call(f32[32,1024]{1,0:T(8,128)} %refs_0_.1, bf16[512,512]{1,0:T(8,128)(2,1)} %constant.46.clone.refs_1_, bf16[544,128]{1,0:T(8,128)(2,1)} %constant.47.clone.refs_2_, f32[8,1024]{1,0:T(8,128)} %constant.48.clone.refs_3_, f32[128,128]{1,0:T(8,128)} %constant.49.clone.refs_4_, ...), custom_call_target="tpu_custom_call" | custom-call | tf_op jit(solution)/shard_map/mlc/pallas_call | solution.py:689
  14.8 0.7 %emit.1 = f32[32,1024]{1,0:T(8,128)} custom-call(f32[32,1024]{1,0:T(8,128)S(1)} %mlc.1.in_ref), custom_call_target="tpu_custom_call" | custom-call | tf_op jit(solution)/shard_map/emit/pallas_call | solution.py:700

commit v2 on v1

--- a/solution.py
+++ b/solution.py
@@ -94,7 +94,7 @@
     picks = [W - 1, W, W + n - 1, W + n]
     a_full = average @ s_l
     b_full = basis.T @ s_l[W : W + n]
-    swapped = [1, 0, 3, 2]
+    order = np.arange(4 * NL).reshape(4, hn, 2).transpose(2, 0, 1).ravel()
     big = {}
 
     folding = np.zeros((4, 4, n, 4, 2 * 4, half))
@@ -111,13 +111,20 @@
     f1 = [inner[p::2, p * half : (p + 1) * half] for p in (0, 1)]
     a1 = [(u_b @ a_full)[p * hb : (p + 1) * hb, p::2] for p in (0, 1)]
     b1 = [b_full[p::2, p::2] for p in (0, 1)]
-    for c, (p, q) in enumerate(CLASSES):
-        big["fwd%d" % c] = np.kron(f1[p], f1[q]).T
-        part = np.zeros((hl * hl, 256))
-        sample, coef = np.kron(a1[p], a1[q]).T, np.kron(b1[p], b1[q]).T
-        part[:, :128] = np.concatenate([sample, coef] if c % 2 == 0 else [coef, sample], axis=1)
-        part[:, 128:192] = np.kron(s_l[picks][:, p::2], b_full[:, q::2]).T
-        big["back%d" % c] = part
+    keep, pick = np.eye(hb), np.concatenate([np.zeros((hn, hb)), np.eye(hn)], axis=1)
+    keep = np.concatenate([keep, np.zeros((hb, hn))], axis=1)
+    for p in (0, 1):
+        big["fy%d" % p] = np.kron(f1[p].T, np.eye(half))
+        high, low = split(np.kron(np.eye(8), f1[p].T))
+        plain["fz%d" % p] = np.concatenate([high, high, low])
+        plain["bz%d" % p] = np.concatenate(
+            split(np.kron(np.eye(8), np.concatenate([a1[p], b1[p]]).T)), axis=1
+        )
+        sample = np.kron(a1[p], keep).T
+        slab = np.kron(s_l[picks][:, p::2], pick).T
+        big["by%d" % p] = np.concatenate(
+            [sample, sample, slab, slab, np.kron(b1[p], pick).T], axis=1
+        )
 
     unfold = u_b.T / 2
     pair = np.kron(unfold, unfold).reshape(blocks * blocks, 2, hb, 2, hb)
@@ -129,10 +136,9 @@
     bm = basis.T @ middle
     lin_x = from_samples(np.kron(bm, bm)).reshape(4 * quad, NL, NL)
     lin = np.zeros((4 * quad, 384))
-    for place, c in enumerate(swapped):
-        p, q = CLASSES[c]
-        lin[:, place * wide : (place + 1) * wide] = lin_x[:, p::2, q::2].reshape(4 * quad, wide)
-    lin[:, 256:320] = from_samples(np.kron(fine[picks], bm))
+    for c, (p, q) in enumerate(CLASSES):
+        lin[:, c * wide : (c + 1) * wide] = lin_x[:, p::2, q::2].reshape(4 * quad, wide)
+    lin[:, 256:320] = from_samples(np.kron(fine[picks], bm))[:, order]
     big["lin"] = lin
     k1 = [(s_n @ u_n.T / 2)[p::2, p * half : (p + 1) * half] for p in (0, 1)]
     big["near"] = np.concatenate([np.kron(k1[p], k1[q]).T for p, q in CLASSES])
@@ -182,14 +188,13 @@
     sb = s_n @ basis
     sbp = np.concatenate([sb[0::2], sb[1::2]])
     facex = np.zeros((4 * wide, n * n))
-    for place, c in enumerate(swapped):
-        p, q = CLASSES[c]
-        facex[place * wide : (place + 1) * wide, c * 256 : c * 256 + 256] = np.kron(
+    for c, (p, q) in enumerate(CLASSES):
+        facex[c * wide : (c + 1) * wide, c * 256 : c * 256 + 256] = np.kron(
             sb[p::2, p::2], sb[q::2, q::2]
         ).T
     big["facex"] = facex
     ends = np.stack([sp[:, 0], sp[:, n - 1], sp[:, 0], sp[:, n - 1]], axis=1)
-    big["facey"] = by_class(ends, sbp)
+    big["facey"] = by_class(ends, sbp)[order]
 
     mu_y, mu_z = eigen_values(ny), eigen_values(nz)
     theta = np.arccosh(1.0 + (mu_y[:, None] + mu_z[None, :]).reshape(1, modes) / 2)
@@ -291,8 +296,7 @@
 
 
 NAMES = [
-    "charge", "fold", "lefts", "sums", "columns",
-    "fwd0", "fwd1", "back0", "fwd2", "back1", "fwd3", "back2", "back3",
+    "charge", "fold", "lefts", "fy0", "fy1", "fz0", "sums", "columns", "bz0", "fz1", "bz1", "by0", "by1",
     "spread", "mine", "lin", "near", "facex", "facey", "toep", "hank", "drop", "far", "unfold",
 ]
 
@@ -364,7 +368,8 @@
 
     groups = [[0, 1, 7, 6], [2, 3, 5, 4]]
     with jax.named_scope("fold"):
-        ready("charge", "fold")
+        with jax.named_scope("f_w"):
+            ready("charge", "fold", "lefts")
         sides = [
             jnp.concatenate([vmem["charge"][:, v * 128 : (v + 1) * 128] for v in group], axis=1)
             for group in groups
@@ -380,32 +385,70 @@
             ],
             axis=1,
         )
-        ready("lefts")
         wide = left_mul("sl", folded)
-        ready("sums", "columns")
-
-    def forward(c):
-        ready("fwd%d" % c)
-        spectrum = right_mul(wide[:, c * 256 : (c + 1) * 256], *table("fwd%d" % c))
-        return spectrum / (column("mul") + vmem["sums"][c : c + 1, :])
-
-    def backward(c, spectrum):
-        ready("back%d" % c)
-        return right_mul(spectrum, *table("back%d" % c))
-
-    with jax.named_scope("classes"):
-        s0 = forward(0)
-        s1 = forward(1)
-        y0 = backward(0, s0)
-        s2 = forward(2)
-        y1 = backward(1, s1)
-        s3 = forward(3)
-        y2 = backward(2, s2)
-        y3 = backward(3, s3)
+
+    half = n + 2 * W
+
+    def along_y(p):
+        pair = [wide[:, c * 256 : (c + 1) * 256] for c in (2 * p, 2 * p + 1)]
+        return right_mul(jnp.concatenate(pair, axis=0), *table("fy%d" % p))
+
+    def along_z(q, lifts):
+        rows = [
+            lift[q * half : (q + 1) * half, k * 128 : (k + 1) * 128]
+            for lift in lifts
+            for k in range(4)
+        ]
+        high, low = halves(jnp.concatenate(rows, axis=0))
+        weights = vmem["fz%d" % q]
+        return mm(jnp.concatenate([high, low], axis=1), weights[0:256]) + mm(high, weights[256:384])
+
+    def divided(q, spectrum):
+        parts = []
+        for p in range(2):
+            for k in range(4):
+                at = (4 * p + k) * half
+                divisor = column("mul") + vmem["sums"][2 * p + q : 2 * p + q + 1, k * 256 : (k + 1) * 256]
+                parts.append(spectrum[at : at + half] / divisor)
+        return jnp.concatenate(parts, axis=0)
+
+    def back_z(q, spectrum):
+        high, low = halves(spectrum)
+        both = mm(jnp.concatenate([high, low], axis=0), vmem["bz%d" % q][...])
+        rows = spectrum.shape[0]
+        return both[:rows, :128] + both[rows:, :128] + both[:rows, 128:]
+
+    def back_y(p, drops):
+        rows = []
+        for drop in drops:
+            parts = [drop[(4 * p + k) * half : (4 * p + k + 1) * half] for k in range(4)]
+            rows.append(jnp.concatenate(parts, axis=1))
+        both = right_mul(jnp.concatenate(rows, axis=0), *table("by%d" % p))
+        return both[:half], both[half:]
+
+    with jax.named_scope("k_wy"):
+        ready("fy0", "fy1")
+    with jax.named_scope("k_y"):
+        lifts = [along_y(0), along_y(1)]
+    with jax.named_scope("k_wz"):
+        ready("fz0", "fz1", "sums", "columns")
+    with jax.named_scope("k_z"):
+        up0 = along_z(0, lifts)
+        up1 = along_z(1, lifts)
+    with jax.named_scope("k_d"):
+        up0 = divided(0, up0)
+        up1 = divided(1, up1)
+    with jax.named_scope("k_wb"):
+        ready("bz0", "bz1", "by0", "by1")
+    with jax.named_scope("k_bz"):
+        drops = [back_z(0, up0), back_z(1, up1)]
+    with jax.named_scope("k_by"):
+        y0, y1 = back_y(0, drops)
+        y2, y3 = back_y(1, drops)
     with jax.named_scope("spread"):
-        first = lax.broadcasted_iota(jnp.int32, (n + 2 * W, 128), 1) < 64
+        lane = lax.broadcasted_iota(jnp.int32, (half, 128), 1)
         sample = jnp.concatenate(
-            [jnp.where(first, u[:, :128], v[:, :128]) for u, v in ((y0, y1), (y2, y3))], axis=1
+            [jnp.where(lane < 64, u[:, :128], v[:, :128]) for u, v in ((y0, y1), (y2, y3))], axis=1
         )
         ready("spread", "mine")
         modes = near_ref.shape[-1]
@@ -486,12 +529,22 @@
 
     with jax.named_scope("lin"):
         ready("lin")
-        coef = jnp.concatenate(
-            [jnp.where(first, v[:, :128], u[:, :128]) for u, v in ((y0, y1), (y2, y3))], axis=1
-        )
-        slab = y0[:, 128:] + y1[:, 128:] + y2[:, 128:] + y3[:, 128:]
+        coef = jnp.concatenate([u[:, 128:] for u in (y0, y1, y2, y3)], axis=1)
+        slab = jnp.where(lane < 32, y0[:, 128:] + y2[:, 128:], y1[:, 128:] + y3[:, 128:])
         flat = right_mul(left_mul("flat", sample), *table("lin"))
-        cx = left_mul("picks", coef)[0:8] - flat[0:8, 0:256]
+        coef = left_mul("picks", coef)[0:8]
+        cx = jnp.concatenate(
+            [
+                jnp.where(
+                    lane[0:8] < 64,
+                    pltpu.roll(coef[:, c * 128 : (c + 1) * 128], 64, 1),
+                    coef[:, (c + 1) * 128 : (c + 2) * 128],
+                )
+                for c in (0, 2)
+            ],
+            axis=1,
+        )
+        cx = cx - flat[0:8, 0:256]
         cy = left_mul("coefs", slab) - flat[8:24, 256:384]
         cx_ref[...] = cx
         cy_ref[...] = cy
@@ -557,7 +610,7 @@
         ends = right_mul(ends, *table("facex"))
         spectrum = spectrum + column("ends")[:, 0:1] * ends[0:1]
         spectrum = spectrum + column("ends")[:, 1:2] * ends[1:2]
-        group = lax.broadcasted_iota(jnp.int32, (16, 128), 1) // 16
+        group = jnp.where(lane[0:16] < 64, lax.rem(lane[0:16], 32) // 8, 4)
         total = jnp.where((group == 0) | (group == 3), cy, 0.0)
         total = total + jnp.where((group == 2) & (b > 0), ry_ref[0], 0.0)
         total = total + jnp.where((group == 1) & (b < n_gy - 1), ry_ref[1], 0.0)

time: 15.6 us -> 14.1 us (0.904)
  Pallas kernels: 15.5 us -> 13.9 us
    pallas_call x1, Pallas kernels: 14.8 us -> 13.3 us  [body(): pl.pallas_call(functools.partial(kernel, column_places, spots, n_gx, n_gy...]
where the time goes in v2:
time: 14.1 us; the launch traced here: 13.9 us
  Pallas kernels  13.9 us (99%)
    pallas_call x1, Pallas kernels, body(): pl.pallas_call(functools.partial(kernel, column_places, spots, n_gx, n_gy...  13.3 us
    pallas_call x1, Pallas kernels, body(): pl.pallas_call(emit, out_shape=jax.ShapeDtypeStruct(charge.shape, charge....  0.67 us

profile of v2, /device:TPU:0, one launch (start us, length us, event | category | flops | bytes accessed | tf_op | source)
XLA Modules:
  0.0 13.9 jit_solution(9867452962110390222)
XLA Ops:
  0.0 13.3 %mlc.1.in_ref = f32[32,1024]{1,0:T(8,128)S(1)} custom-call(f32[32,1024]{1,0:T(8,128)} %refs_0_.1, bf16[512,512]{1,0:T(8,128)(2,1)} %constant.46.clone.refs_1_, bf16[544,128]{1,0:T(8,128)(2,1)} %constant.47.clone.refs_2_, bf16[2,256,512]{2,1,0:T(8,128)(2,1)} %constant.48.clone.refs_3_, bf16[2,256,512]{2,1,0:T(8,128)(2,1)} %constant.49.clone.refs_4_, ...), custom_call_target="tpu_custom_call" | custom-call | tf_op jit(solution)/shard_map/mlc/pallas_call | solution.py:742
  13.3 0.7 %emit.1 = f32[32,1024]{1,0:T(8,128)} custom-call(f32[32,1024]{1,0:T(8,128)S(1)} %mlc.1.in_ref), custom_call_target="tpu_custom_call" | custom-call | tf_op jit(solution)/shard_map/emit/pallas_call | solution.py:753

commit v3 on v2

v3 whole, which is shorter than its diff:
```python
import functools

import jax
import jax.numpy as jnp
import ml_dtypes
import numpy as np
from jax import lax
from jax.experimental import pallas as pl
from jax.experimental.pallas import tpu as pltpu
from jax.sharding import PartitionSpec as P

P_SIZE = 32
W = 16
Q = 4
NL = 16
CLASSES = [(0, 0), (0, 1), (1, 0), (1, 1)]
MESH = pl.DeviceIdType.MESH


def sine_table(length):
    counter = np.arange(length) + 1
    return np.sin(np.pi * np.outer(counter, counter) / (length + 1))


def eigen_values(length):
    return 2.0 - 2.0 * np.cos(np.pi * (np.arange(length) + 1) / (length + 1))


def interp_table(fine_start, fine_count, coarse_start, coarse_count, ratio):
    fine_pos = np.arange(fine_count) + fine_start
    coarse_pos = np.arange(coarse_count) + coarse_start
    numerator = 2 * fine_pos - (ratio - 1)
    lower = numerator // (2 * ratio)
    weight = ((numerator - 2 * ratio * lower) / (2 * ratio))[:, None]
    below = coarse_pos[None, :] == lower[:, None]
    above = coarse_pos[None, :] == lower[:, None] + 1
    return below * (1.0 - weight) + above * weight


def legendre_basis(length, count):
    points = (2.0 * np.arange(length) + 1.0) / length - 1.0
    columns = [np.ones_like(points), points]
    for degree in range(2, count):
        columns.append(
            ((2 * degree - 1) * points * columns[-1] - (degree - 1) * columns[-2]) / degree
        )
    result = []
    for vector in columns[:count]:
        for passes in range(2):
            for earlier in result:
                vector = vector - np.sum(earlier * vector) * earlier
        result.append(vector / np.sqrt(np.sum(vector * vector)))
    return np.stack(result, axis=1)


def fold(length):
    half = length // 2
    eye = np.eye(length)
    return np.concatenate([eye[:half] + eye[::-1][:half], eye[:half] - eye[::-1][:half]])


def split(table):
    high = table.astype(ml_dtypes.bfloat16)
    low = (table - high.astype(np.float64)).astype(ml_dtypes.bfloat16)
    return high, low


@functools.lru_cache(maxsize=None)
def tables(n_gx, n_gy):
    n, length, cells = P_SIZE, P_SIZE + 2 * W, P_SIZE // Q
    blocks, margin = length // Q, W // Q
    half, hl, hb, hn = n // 2, length // 2, blocks // 2, NL // 2
    quad, wide = hb * hb, hn * hn
    nx, ny, nz = n_gx * cells, n_gy * cells, cells
    modes = ny * nz
    s_l, s_n = sine_table(length), sine_table(n)
    u_n, u_b = fold(n), fold(blocks)
    basis = legendre_basis(n, NL)
    average = np.kron(np.eye(blocks), np.full((1, Q), 1.0 / Q))
    fine = interp_table(0, length, 0, blocks, Q)
    middle = fine[W : W + n]
    picks = [W - 1, W, W + n - 1, W + n]
    a_full = average @ s_l
    b_full = basis.T @ s_l[W : W + n]
    order = np.arange(4 * NL).reshape(4, hn, 2).transpose(2, 0, 1).ravel()
    big = {}

    folding = np.zeros((2, 4, n, 2, 2, 4, half))
    for p, q in CLASSES:
        for y4 in range(4):
            piece = u_n[q * half : (q + 1) * half].T
            folding[0, y4, :, p, q, y4, :] = piece
            folding[1, y4, :, p, q, 3 - y4, :] = piece if p == 0 else -piece
    plain = {"fold": folding.reshape(256, 256)}
    folding = np.zeros((4, 4, n, 4, 2 * 4, half))
    for c, (p, q) in enumerate(CLASSES):
        for vi in range(4):
            for y4 in range(4):
                il = [y4, 4 + y4, 3 - y4, 7 - y4][vi]
                sign = -1.0 if vi > 1 and p == 1 else 1.0
                folding[vi, y4, :, c, il, :] = sign * u_n[q * half : (q + 1) * half].T
    folding = folding.reshape(4 * 128, 4 * 128)
    plain["unfold"] = folding.T

    inner = s_l[:, W : W + n] @ u_n.T / 2
    f1 = [inner[p::2, p * half : (p + 1) * half] for p in (0, 1)]
    a1 = [(u_b @ a_full)[p * hb : (p + 1) * hb, p::2] for p in (0, 1)]
    b1 = [b_full[p::2, p::2] for p in (0, 1)]
    keep, pick = np.eye(hb), np.concatenate([np.zeros((hn, hb)), np.eye(hn)], axis=1)
    keep = np.concatenate([keep, np.zeros((hb, hn))], axis=1)
    for p in (0, 1):
        big["fy%d" % p] = np.kron(f1[p].T, np.eye(half))
        high, low = split(np.kron(np.eye(8), f1[p].T))
        plain["fz%d" % p] = np.concatenate([high, high])
        plain["gz%d" % p] = low
        plain["bz%d" % p] = np.concatenate(
            split(np.kron(np.eye(8), np.concatenate([a1[p], b1[p]]).T)), axis=1
        )
        sample = np.kron(a1[p], keep).T
        slab = np.kron(s_l[picks][:, p::2], pick).T
        big["by%d" % p] = np.concatenate(
            [sample, sample, slab, slab, np.kron(b1[p], pick).T], axis=1
        )

    unfold = u_b.T / 2
    pair = np.kron(unfold, unfold).reshape(blocks * blocks, 2, hb, 2, hb)

    def from_samples(table):
        folded = np.einsum("os,spaqb->pqabo", table, pair)
        return folded.reshape(4 * quad, table.shape[0])

    bm = basis.T @ middle
    lin_x = from_samples(np.kron(bm, bm)).reshape(4 * quad, NL, NL)
    lin = np.zeros((4 * quad, 384))
    for c, (p, q) in enumerate(CLASSES):
        lin[:, c * wide : (c + 1) * wide] = lin_x[:, p::2, q::2].reshape(4 * quad, wide)
    lin[:, 256:320] = from_samples(np.kron(fine[picks], bm))[:, order]
    big["lin"] = lin
    k1 = [(s_n @ u_n.T / 2)[p::2, p * half : (p + 1) * half] for p in (0, 1)]
    for c, (p, q) in enumerate(CLASSES):
        big["near%d" % c] = np.kron(k1[p], k1[q]).T
    r1 = [(u_n @ s_n / 2)[p * half : (p + 1) * half, p::2] for p in (0, 1)]
    for c, (p, q) in enumerate(CLASSES):
        big["far%d" % c] = np.kron(r1[p], r1[q]).T

    second = 2 * np.eye(blocks) - np.eye(blocks, k=1) - np.eye(blocks, k=-1)
    s_y, s_z = sine_table(ny), sine_table(nz)
    proj_z = np.zeros((nz, blocks))
    proj_z[:, margin : margin + cells] = s_z
    edge = interp_table(-1, n + 2, -1, cells + 2, Q)
    depth = interp_table(0, n, 0, cells, Q)
    lateral = edge[1 : n + 1]
    s_ext = np.zeros((ny + 2, ny))
    s_ext[1:-1] = s_y
    sp = np.concatenate([s_n[0::2], s_n[1::2]])
    deep = sp @ depth @ s_z

    def by_class(first, second_table):
        parts = []
        for p, q in CLASSES:
            parts.append(
                np.kron(first[p * half : (p + 1) * half], second_table[q * half : (q + 1) * half])
            )
        return np.concatenate(parts).T

    factor = (2.0 / (ny + 1)) * (2.0 / (nz + 1))
    spread, drop = [], []
    for b in range(n_gy):
        proj_y = np.zeros((ny, blocks))
        for j in range(blocks):
            at = j + b * cells - margin
            if 0 <= at < ny:
                proj_y[:, j] = s_y[:, at]
        flat = np.kron(proj_y, proj_z)
        curved = np.kron(proj_y @ second, proj_z) + np.kron(proj_y, proj_z @ second)
        spread.append(
            factor * np.concatenate([from_samples(curved), from_samples(flat)], axis=1)
        )
        local_s = s_ext[b * cells : b * cells + cells + 2]
        rim = np.outer(sp[:, 0], edge[0] @ local_s) + np.outer(sp[:, n - 1], edge[n + 1] @ local_s)
        drop.append(
            np.concatenate([by_class(sp @ lateral @ local_s, deep), by_class(rim, deep)])
        )
    big["spread"] = np.stack(spread)
    big["drop"] = np.stack(drop)
    sb = s_n @ basis
    sbp = np.concatenate([sb[0::2], sb[1::2]])
    facex = np.zeros((4 * wide, n * n))
    for c, (p, q) in enumerate(CLASSES):
        facex[c * wide : (c + 1) * wide, c * 256 : c * 256 + 256] = np.kron(
            sb[p::2, p::2], sb[q::2, q::2]
        ).T
    big["facex"] = facex
    ends = np.stack([sp[:, 0], sp[:, n - 1], sp[:, 0], sp[:, n - 1]], axis=1)
    big["facey"] = by_class(ends, sbp)[order]

    mu_y, mu_z = eigen_values(ny), eigen_values(nz)
    theta = np.arccosh(1.0 + (mu_y[:, None] + mu_z[None, :]).reshape(1, modes) / 2)
    below = 2 * np.sinh(theta) * (1.0 - np.exp(-2 * theta * (nx + 1)))
    apart = np.abs(np.arange(48) - 20)[:, None]
    toep = (np.exp(-theta * apart) + np.exp(-theta * np.maximum(2 * (nx + 1) - apart, 0))) / below
    total = (np.arange(2 * nx + 32) - 13)[:, None]
    hank = np.exp(-theta * np.maximum(total + 2, 0)) + np.exp(-theta * np.maximum(2 * nx - total, 0))
    hank = hank / below

    u12 = np.zeros((64, 16))
    u12[:32, :10] = np.outer(s_n[:, 0], edge[0]) + np.outer(s_n[:, n - 1], edge[n + 1])
    u12[32:, :10] = s_n @ lateral
    place = np.arange(n_gx)
    mine = []
    for a in range(n_gx):
        rank = np.arange(16)[:, None]
        at = cells * a - margin + rank
        inside = (at >= 0) & (at < nx)
        rightward = inside * np.exp(-theta * (15 - rank)) * (1 - np.exp(-2 * theta * (at + 1) * inside))
        leftward = inside * np.exp(-theta * rank) * (1 - np.exp(-2 * theta * (nx - at) * inside))
        row = np.arange(16)[:, None]
        x = cells * a - 1 + row
        used = row < cells + 2
        falling = used * np.exp(-theta * row) * (1 - np.exp(-2 * theta * np.maximum(nx - x, 0))) / below
        rising = (
            used
            * np.exp(-theta * np.maximum(cells + 1 - row, 0))
            * (1 - np.exp(-2 * theta * (x + 1)))
            / below
        )
        away = (a - place)[:, None]
        before = (away >= 2) * np.exp(-theta * np.maximum(cells * away - 12, 0))
        after = (away <= -2) * np.exp(-theta * np.maximum(-cells * away - 12, 0))
        mine.append(
            np.concatenate(
                [
                    rightward,
                    leftward,
                    u12 @ falling,
                    u12 @ rising,
                    toep,
                    hank[2 * cells * a : 2 * cells * a + 48],
                    before,
                    after,
                ]
            )
        )
    mu_l, mu_n = eigen_values(length), eigen_values(n)
    reciprocal = []
    for q in (0, 1):
        for p in (0, 1):
            pair_sum = (mu_l[p::2][:, None] + mu_l[q::2][None, :]).reshape(4, 1, 256)
            reciprocal.append((1.0 / (mu_l[None, :, None] + pair_sum)).reshape(4 * length, 256))
    for p, q in CLASSES:
        pair_sum = (mu_n[p::2][:, None] + mu_n[q::2][None, :]).reshape(1, 256)
        reciprocal.append((2.0 / (n + 1)) ** 3 / (mu_n[:, None] + pair_sum))
    ends = np.zeros((n, 256))
    ends[:, :2] = s_n[:, [0, n - 1]]
    reciprocal.append(ends)

    scale = (2.0 / (length + 1)) ** 3
    flat = np.zeros((32, length))
    flat[:4] = fine[picks] @ a_full * scale
    flat[16:] = bm @ a_full * scale
    lefts = {
        "sl": s_l[:, W : W + n],
        "source": np.concatenate([a_full, second @ a_full], axis=1) * scale,
        "flat": flat,
        "picks": np.concatenate([s_l[picks] * scale, np.zeros((12, length))]),
        "coefs": b_full * scale,
        "sn": s_n,
        "u12": u12,
        "sb": sb,
    }
    big.update(lefts)
    singles = {
        "mine": np.stack(mine).astype(np.float32),
        "recip": np.concatenate(reciprocal).astype(np.float32),
    }
    places = {}
    for group, names in GROUPS.items():
        packs, row = [], 0
        for name in names:
            if name in plain:
                parts = [plain[name].astype(ml_dtypes.bfloat16)]
            else:
                parts = split(big[name])
            depth, width = parts[0].shape[-2:]
            place = {"left": (row, depth, width)}
            lefty = name in lefts
            step = 256 if not lefty else width
            tiles = []
            for part in parts:
                start = row
                for at in range(0, width, step):
                    tile = np.zeros(part.shape[:-1] + (256,), ml_dtypes.bfloat16)
                    piece = part[..., at : at + step]
                    tile[..., : piece.shape[-1]] = piece
                    packs.append(tile)
                    tiles.append((row, depth))
                    row += depth
            count = len(tiles) // len(parts)
            place["tiles"] = [tiles[k * count : (k + 1) * count] for k in range(len(parts))]
            places[name] = (group, place)
        most = max(tile.ndim for tile in packs)
        if most == 3:
            packs = [np.broadcast_to(tile, (n_gy,) + tile.shape[-2:]) for tile in packs]
        singles[group] = np.concatenate(packs, axis=-2)
    return singles, places


GROUPS = {
    "first": ["fold", "sl"],
    "upy": ["fy0", "fy1"],
    "upz": ["fz0", "gz0", "fz1", "gz1", "bz0", "bz1"],
    "downy": ["by0", "by1", "source"],
    "spread": ["spread"],
    "side": ["flat", "picks", "coefs", "sn", "sb", "u12", "lin"]
    + ["near%d" % c for c in range(4)]
    + ["facex", "facey"],
    "drop": ["drop"],
    "last": ["far%d" % c for c in range(4)] + ["unfold"],
}
NAMES = ["charge", "first", "upy", "upz", "recip", "downy", "spread", "mine", "side", "drop", "last"]


def halves(value):
    high = value.astype(jnp.bfloat16)
    return high, (value - high.astype(jnp.float32)).astype(jnp.bfloat16)


def mm(left, right):
    return jnp.dot(left, right, preferred_element_type=jnp.float32)


def window(name, shape):
    return shape[1:] if name in ("spread", "drop", "mine") else shape


def kernel(places, n_gx, n_gy, *refs):
    count = len(NAMES)
    hbm = dict(zip(NAMES, refs[:count]))
    out_ref = refs[count]
    vmem = dict(zip(NAMES, refs[count + 1 : 2 * count + 1]))
    (
        fold_ref, w_ref, z_ref, b_ref, y_ref,
        mom_ref, far_ref, near_ref, cx_ref, cy_ref, rx_ref, ry_ref, tally_ref,
        load_sem, f_send, f_recv, p_send, p_recv,
    ) = refs[2 * count + 1 :]
    ndev = n_gx * n_gy
    a = lax.axis_index("gx")
    b = lax.axis_index("gy")
    me = a * n_gy + b
    n, cells = P_SIZE, P_SIZE // Q
    half = n + 2 * W
    modes = near_ref.shape[-1]

    loads = {}
    for i, name in enumerate(NAMES):
        source = hbm[name]
        if name in ("spread", "drop"):
            source = source.at[b]
        if name == "mine":
            source = source.at[a]
        loads[name] = pltpu.make_async_copy(source, vmem[name], load_sem.at[i])
        loads[name].start()

    barrier = pltpu.get_barrier_semaphore()

    def greet(r, carry):
        peer = lax.rem(me + r, ndev)
        pl.semaphore_signal(
            barrier, inc=1, device_id=(peer // n_gy, lax.rem(peer, n_gy)), device_id_type=MESH
        )
        return carry

    with jax.named_scope("greet"):
        lax.fori_loop(1, ndev, greet, 0)

    def tile(name, part, i):
        group, place = places[name]
        row, depth = place["tiles"][part][i]
        return vmem[group][row : row + depth, :]

    def table(name, part):
        count = len(places[name][1]["tiles"][part])
        return jnp.concatenate([tile(name, part, i) for i in range(count)], axis=1)

    def right_mul(high, low, name):
        rows = high.shape[0]
        both = mm(jnp.concatenate([high, low], axis=0), table(name, 0))
        return both[:rows] + both[rows:] + mm(high, table(name, 1))

    def left_mul(name, high, low):
        group, place = places[name]
        row, rows, cols = place["left"]
        both = mm(vmem[group][row : row + 2 * rows, 0:cols], high)
        return both[:rows] + both[rows:] + mm(vmem[group][row : row + rows, 0:cols], low)

    groups = [[0, 1, 7, 6], [2, 3, 5, 4]]
    with jax.named_scope("w_charge"):
        loads["charge"].wait()
    with jax.named_scope("w_first"):
        loads["first"].wait()
    with jax.named_scope("fold"):
        charge = vmem["charge"]
        pairs = [
            jnp.concatenate([charge[:, v * 128 : (v + 1) * 128] for v in (u, 7 - u)], axis=1)
            for u in range(4)
        ]
        high, low = halves(jnp.concatenate(pairs, axis=0))
        both = mm(jnp.concatenate([high, low], axis=0), tile("fold", 0, 0))
        both = both[: 4 * n] + both[4 * n :]
        lane = lax.broadcasted_iota(jnp.int32, (half, 128), 1)
        folded = []
        for p in range(2):
            rows = [both[v * n : (v + 1) * n, p * 128 : (p + 1) * 128] for v in range(4)]
            turn = [pltpu.roll(row, 64, 1) for row in rows]
            left = lane[:n] < 64
            folded += [jnp.where(left, rows[v], turn[v + 1]) for v in (0, 2)]
            folded += [jnp.where(left, turn[v], rows[v + 1]) for v in (0, 2)]
        folded = halves(jnp.concatenate(folded, axis=1))
        fold_ref[0] = folded[0]
        fold_ref[1] = folded[1]
        wide = halves(left_mul("sl", *folded))
        for c in range(4):
            at = slice(c * 256, (c + 1) * 256)
            q = c % 2
            w_ref[c // 2, q * half : (q + 1) * half] = wide[0][:, at]
            w_ref[c // 2, (2 + q) * half : (3 + q) * half] = wide[1][:, at]
    with jax.named_scope("w_upy"):
        loads["upy"].wait()
    with jax.named_scope("upy"):
        for p in range(2):
            name = "fy%d" % p
            both = mm(w_ref[p], table(name, 0))
            lift = both[: 2 * half] + both[2 * half :] + mm(w_ref[p, 0 : 2 * half], table(name, 1))
            high, low = halves(lift)
            for q in range(2):
                for k in range(4):
                    at = (4 * p + k) * half
                    rows, lanes = slice(q * half, (q + 1) * half), slice(k * 128, (k + 1) * 128)
                    z_ref[q, at : at + half, 0:128] = high[rows, lanes]
                    z_ref[q, at : at + half, 128:256] = low[rows, lanes]
    with jax.named_scope("w_upz"):
        loads["upz"].wait()
        loads["recip"].wait()
    with jax.named_scope("upz"):
        rows = 8 * half
        for q in range(2):
            up = mm(z_ref[q], tile("fz%d" % q, 0, 0)) + mm(z_ref[q, :, 0:128], tile("gz%d" % q, 0, 0))
            high, low = halves(up * vmem["recip"][q * rows : (q + 1) * rows])
            b_ref[q, 0:rows] = high
            b_ref[q, rows : 2 * rows] = low
    with jax.named_scope("downz"):
        for q in range(2):
            both = mm(b_ref[q], tile("bz%d" % q, 0, 0))
            high, low = halves(both[:rows, :128] + both[rows:, :128] + both[:rows, 128:])
            for p in range(2):
                for k in range(4):
                    at, lanes = (4 * p + k) * half, slice(k * 128, (k + 1) * 128)
                    y_ref[p, q * half : (q + 1) * half, lanes] = high[at : at + half]
                    y_ref[p, (2 + q) * half : (3 + q) * half, lanes] = low[at : at + half]
    with jax.named_scope("w_downy"):
        loads["downy"].wait()
    with jax.named_scope("downy"):
        ys = []
        for p in range(2):
            name = "by%d" % p
            both = mm(y_ref[p], tile(name, 0, 0))
            both = both[: 2 * half] + both[2 * half :] + mm(y_ref[p, 0 : 2 * half], tile(name, 1, 0))
            ys += [both[:half], both[half:]]
        y0, y1, y2, y3 = ys
    with jax.named_scope("w_spread"):
        loads["spread"].wait()
        loads["mine"].wait()
    with jax.named_scope("spread"):
        sample = halves(
            jnp.concatenate(
                [jnp.where(lane < 64, u[:, :128], v[:, :128]) for u, v in ((y0, y1), (y2, y3))],
                axis=1,
            )
        )
        high, low = halves(right_mul(*sample, "spread"))
        packet = left_mul(
            "source",
            jnp.concatenate([high[:, :modes], high[:, modes:]], axis=0),
            jnp.concatenate([low[:, :modes], low[:, modes:]], axis=0),
        )
        near_ref[n_gy + b] = packet
        mine = vmem["mine"]
        rightward = jnp.sum(packet * mine[0:16], axis=0, keepdims=True)
        leftward = jnp.sum(packet * mine[16:32], axis=0, keepdims=True)
        for g in range(modes // 128):
            mom_ref[g, 0:1] = rightward[:, g * 128 : (g + 1) * 128]
            mom_ref[g, 1:2] = leftward[:, g * 128 : (g + 1) * 128]

    with jax.named_scope("barrier"):
        pl.semaphore_wait(barrier, ndev - 1)

    def remote(source, target, send, recv, device):
        return pltpu.make_async_remote_copy(
            src_ref=source,
            dst_ref=target,
            send_sem=send,
            recv_sem=recv,
            device_id=device,
            device_id_type=MESH,
        )

    def start_far(r, carry):
        d = n_gx - r
        for j in range(n_gy):
            for row, other, fine in ((0, a + d, a + d < n_gx), (1, a - d, a >= d)):

                @pl.when(fine)
                def _():
                    remote(
                        mom_ref.at[:, pl.ds(row, 1)],
                        far_ref.at[b, :, pl.ds(a, 1)],
                        f_send,
                        f_recv,
                        (other, j),
                    ).start()

        return carry

    with jax.named_scope("send"):
        lax.fori_loop(1, n_gx - 1, start_far, 0)
        for step in (0, 1, 2):
            for j in range(n_gy):
                other = a + step - 1
                fine = (other >= 0) & (other < n_gx)
                if step == 1:
                    fine = b != j

                @pl.when(fine)
                def _():
                    remote(
                        near_ref.at[n_gy + b],
                        near_ref.at[(2 - step) * n_gy + b],
                        p_send,
                        p_recv,
                        (other, j),
                    ).start()

    with jax.named_scope("w_side"):
        loads["side"].wait()
    with jax.named_scope("lin"):
        coef = halves(jnp.concatenate([u[:, 128:] for u in (y0, y1, y2, y3)], axis=1))
        slab = halves(jnp.where(lane < 32, y0[:, 128:] + y2[:, 128:], y1[:, 128:] + y3[:, 128:]))
        flat = right_mul(*halves(left_mul("flat", *sample)), "lin")
        coef = left_mul("picks", *coef)[0:8]
        cx = jnp.concatenate(
            [
                jnp.where(
                    lane[0:8] < 64,
                    pltpu.roll(coef[:, c * 128 : (c + 1) * 128], 64, 1),
                    coef[:, (c + 1) * 128 : (c + 2) * 128],
                )
                for c in (0, 2)
            ],
            axis=1,
        )
        cx = cx - flat[0:8, 0:256]
        cy = left_mul("coefs", *slab) - flat[16:32, 256:384]
        cx_ref[...] = cx
        cy_ref[...] = cy

    upper, lower = lax.rem(b + 1, n_gy), lax.rem(b + n_gy - 1, n_gy)
    with jax.named_scope("sendc"):

        @pl.when(a < n_gx - 1)
        def _():
            remote(
                cx_ref.at[pl.ds(2, 1)], rx_ref.at[pl.ds(0, 1)], p_send, p_recv, (a + 1, b)
            ).start()

        @pl.when(a > 0)
        def _():
            remote(
                cx_ref.at[pl.ds(1, 1)], rx_ref.at[pl.ds(1, 1)], p_send, p_recv, (a - 1, b)
            ).start()

        remote(cy_ref, ry_ref.at[0], p_send, p_recv, (a, upper)).start()
        remote(cy_ref, ry_ref.at[1], p_send, p_recv, (a, lower)).start()

    with jax.named_scope("near"):
        narrow = halves(left_mul("sn", fold_ref[0], fold_ref[1]))
        spectrum = []
        for c in range(4):
            at = slice(c * 256, (c + 1) * 256)
            spectrum.append(right_mul(narrow[0][:, at], narrow[1][:, at], "near%d" % c))
        spectrum = jnp.concatenate(spectrum, axis=1)

    edge = (a == 0) | (a == n_gx - 1)
    inner = jnp.logical_not(edge)

    def settle_near(sides):
        lines = 16 * (modes // 128) * ((1 + sides) * n_gy - 1) + 2 * sides + 32
        block = tally_ref.at[pl.ds(0, lines)]
        remote(block, block, p_send, p_recv, (a, b)).wait()

    with jax.named_scope("wait_p"):

        @pl.when(edge)
        def _():
            settle_near(1)

        @pl.when(inner)
        def _():
            settle_near(2)

    with jax.named_scope("face"):
        from_left = jnp.where(a > 0, rx_ref[0:1], 0.0)
        from_right = jnp.where(a < n_gx - 1, rx_ref[1:2], 0.0)
        ends = jnp.concatenate(
            [cx[0:1] + from_left, cx[3:4] + from_right, jnp.zeros((14, cx.shape[1]), jnp.float32)]
        )
        ends = right_mul(*halves(ends), "facex")
        fine = 16 * half
        column = vmem["recip"][fine + 4 * n : fine + 5 * n, 0:2]
        spectrum = spectrum + column[:, 0:1] * ends[0:1] + column[:, 1:2] * ends[1:2]
        group = jnp.where(lane[0:16] < 64, lax.rem(lane[0:16], 32) // 8, 4)
        total = jnp.where((group == 0) | (group == 3), cy, 0.0)
        total = total + jnp.where((group == 2) & (b > 0), ry_ref[0], 0.0)
        total = total + jnp.where((group == 1) & (b < n_gy - 1), ry_ref[1], 0.0)
        total = left_mul("sb", *halves(total))[:, 0:64]
        spectrum = spectrum + right_mul(*halves(total), "facey")
    with jax.named_scope("green"):
        row = lax.broadcasted_iota(jnp.int32, (8, modes), 0)

        def gathered(step):
            value = near_ref[step * n_gy]
            for j in range(1, n_gy):
                value = value + near_ref[step * n_gy + j]
            return value

        past = jnp.where(a > 0, gathered(0), 0.0)
        here = gathered(1)
        next_ = jnp.where(a < n_gx - 1, gathered(2), 0.0)
        source = jnp.concatenate(
            [
                jnp.where((row >= 4) | (a > 1), past[0:8], 0.0),
                past[8:16] + jnp.where((row >= 4) | (a > 0), here[0:8], 0.0),
                jnp.where((row < 4) | (a < n_gx - 1), here[8:16] + next_[0:8], 0.0),
                jnp.where((row < 4) | (a < n_gx - 2), next_[8:16], 0.0),
            ]
        )
        values = []
        for i in range(cells + 2):
            influence = mine[169 - i : 201 - i] - mine[208 + i : 240 + i]
            values.append(jnp.sum(influence * source, axis=0, keepdims=True))
        values.append(jnp.zeros((16 - len(values), modes), jnp.float32))
        lifted = left_mul("u12", *halves(jnp.concatenate(values, axis=0)))

    with jax.named_scope("w_last"):
        loads["drop"].wait()
        loads["last"].wait()

    def settle_far(each):
        block = far_ref.at[:, :, pl.ds(0, each)]
        remote(block, block, f_send, f_recv, (a, b)).wait()

    with jax.named_scope("wait_f"):

        @pl.when(edge)
        def _():
            settle_far(n_gx - 2)

        @pl.when(inner)
        def _():
            settle_far(n_gx - 3)

    with jax.named_scope("final"):
        origin = lax.broadcasted_iota(jnp.int32, (n_gx, modes), 0)
        before = jnp.zeros((n_gx, modes), jnp.float32)
        after = before
        for j in range(n_gy):
            sent = jnp.concatenate([far_ref[j, g] for g in range(modes // 128)], axis=1)
            before = before + jnp.where(origin <= a - 2, sent, 0.0)
            after = after + jnp.where(origin >= a + 2, sent, 0.0)
        before = jnp.sum(before * mine[256 : 256 + n_gx], axis=0, keepdims=True)
        after = jnp.sum(after * mine[256 + n_gx : 256 + 2 * n_gx], axis=0, keepdims=True)
        lifted = lifted + mine[32:96] * before + mine[96:160] * after
        lifted = halves(jnp.concatenate([lifted[:n], lifted[n:]], axis=1))
        inverse = jnp.concatenate(
            [vmem["recip"][fine + c * n : fine + (c + 1) * n] for c in range(4)], axis=1
        )
        spectrum = (spectrum + right_mul(*lifted, "drop")) * inverse
        high, low = halves(left_mul("sn", *halves(spectrum)))
        parts = []
        for c in range(4):
            at = slice(c * 256, (c + 1) * 256)
            parts.append(right_mul(high[:, at], low[:, at], "far%d" % c))
    with jax.named_scope("unfold"):
        sides = [
            jnp.concatenate([part[:, s * 128 : (s + 1) * 128] for part in parts], axis=1)
            for s in range(2)
        ]
        high, low = halves(jnp.concatenate(sides, axis=0))
        stacked = jnp.concatenate([high, low], axis=0)
        both = mm(stacked, table("unfold", 0))
        both = both[: 2 * n] + both[2 * n :]
        for s, group in enumerate(groups):
            for i, v in enumerate(group):
                out_ref[:, v * 128 : (v + 1) * 128] = both[
                    s * n : (s + 1) * n, i * 128 : (i + 1) * 128
                ]


def emit(in_ref, out_ref, sem):
    copy = pltpu.make_async_copy(in_ref, out_ref, sem)
    copy.start()
    copy.wait()


def body(n_gx, n_gy, charge):
    singles, places = tables(n_gx, n_gy)
    arrays = [charge] + [jnp.asarray(singles[name]) for name in NAMES[1:]]
    scratch = [
        pltpu.VMEM(window(name, array.shape), array.dtype) for name, array in zip(NAMES, arrays)
    ]
    modes = n_gy * (P_SIZE // Q) ** 2
    half = P_SIZE + 2 * W
    scratch += [
        pltpu.VMEM((2, P_SIZE, 1024), jnp.bfloat16),
        pltpu.VMEM((2, 4 * half, 256), jnp.bfloat16),
        pltpu.VMEM((2, 8 * half, 256), jnp.bfloat16),
        pltpu.VMEM((2, 16 * half, 256), jnp.bfloat16),
        pltpu.VMEM((2, 4 * half, 512), jnp.bfloat16),
        pltpu.VMEM((modes // 128, 8, 128), jnp.float32),
        pltpu.VMEM((n_gy, modes // 128, n_gx, 128), jnp.float32),
        pltpu.VMEM((3 * n_gy, 16, modes), jnp.float32),
        pltpu.VMEM((8, 256), jnp.float32),
        pltpu.VMEM((16, 128), jnp.float32),
        pltpu.VMEM((8, 256), jnp.float32),
        pltpu.VMEM((2, 16, 128), jnp.float32),
        pltpu.VMEM((16 * (modes // 128) * (3 * n_gy - 1) + 40, 128), jnp.float32),
        pltpu.SemaphoreType.DMA((len(NAMES),)),
        pltpu.SemaphoreType.DMA,
        pltpu.SemaphoreType.DMA,
        pltpu.SemaphoreType.DMA,
        pltpu.SemaphoreType.DMA,
    ]
    hbm = pl.BlockSpec(memory_space=pl.ANY)
    vm = pl.BlockSpec(memory_space=pltpu.VMEM)
    solved = pl.pallas_call(
        functools.partial(kernel, places, n_gx, n_gy),
        out_shape=pltpu.VMEM(charge.shape, charge.dtype),
        in_specs=[hbm] * len(NAMES),
        out_specs=vm,
        scratch_shapes=scratch,
        name="mlc",
        compiler_params=pltpu.CompilerParams(
            collective_id=0, has_side_effects=True, vmem_limit_bytes=60 * 1024 * 1024
        ),
    )(*arrays)
    return pl.pallas_call(
        emit,
        out_shape=jax.ShapeDtypeStruct(charge.shape, charge.dtype),
        in_specs=[vm],
        out_specs=hbm,
        scratch_shapes=[pltpu.SemaphoreType.DMA],
        name="emit",
        compiler_params=pltpu.CompilerParams(vmem_limit_bytes=1024 * 1024),
    )(solved)


def solution(mesh):
    run = functools.partial(body, mesh.shape["gx"], mesh.shape["gy"])
    spec = P("gx", "gy")
    return jax.shard_map(run, mesh=mesh, in_specs=(spec,), out_specs=spec, check_vma=False)
```

time: 14.1 us -> 13.7 us (0.972)
  Pallas kernels: 13.9 us -> 13.6 us
    pallas_call x1, Pallas kernels: 13.3 us -> 12.9 us  [body(): pl.pallas_call(functools.partial(kernel, places, n_gx, n_gy), out_shape=p...]
where the time goes in v3:
time: 13.7 us; the launch traced here: 13.6 us
  Pallas kernels  13.6 us (99%)
    pallas_call x1, Pallas kernels, body(): pl.pallas_call(functools.partial(kernel, places, n_gx, n_gy), out_shape=p...  12.9 us
    pallas_call x1, Pallas kernels, body(): pl.pallas_call(emit, out_shape=jax.ShapeDtypeStruct(charge.shape, charge....  0.67 us

profile of v3, /device:TPU:0, one launch (start us, length us, event | category | flops | bytes accessed | tf_op | source)
XLA Modules:
  0.0 13.6 jit_solution(13062662245736838527)
XLA Ops:
  0.0 12.9 %mlc.1.in_ref = f32[32,1024]{1,0:T(8,128)S(1)} custom-call(f32[32,1024]{1,0:T(8,128)} %refs_0_.1, bf16[384,256]{1,0:T(8,128)(2,1)} %constant.20.clone.refs_1_, bf16[2048,256]{1,0:T(8,128)(2,1)} %constant.21.clone.refs_2_, bf16[1280,256]{1,0:T(8,128)(2,1)} %constant.22.clone.refs_3_, f32[1184,256]{1,0:T(8,128)} %constant.23.clone.refs_4_, ...), custom_call_target="tpu_custom_call" | custom-call | tf_op jit(solution)/shard_map/mlc/pallas_call | solution.py:744
  12.9 0.7 %emit.1 = f32[32,1024]{1,0:T(8,128)} custom-call(f32[32,1024]{1,0:T(8,128)S(1)} %mlc.1.in_ref), custom_call_target="tpu_custom_call" | custom-call | tf_op jit(solution)/shard_map/emit/pallas_call | solution.py:755

commit v4 on v3

--- a/solution.py
+++ b/solution.py
@@ -118,8 +118,9 @@
         )
         sample = np.kron(a1[p], keep).T
         slab = np.kron(s_l[picks][:, p::2], pick).T
-        big["by%d" % p] = np.concatenate(
-            [sample, sample, slab, slab, np.kron(b1[p], pick).T], axis=1
+        plain["by%d" % p] = np.concatenate(split(np.concatenate([sample, sample], axis=1)), axis=1)
+        plain["cy%d" % p] = np.concatenate(
+            split(np.concatenate([slab, slab, np.kron(b1[p], pick).T], axis=1)), axis=1
         )
 
     unfold = u_b.T / 2
@@ -245,8 +246,9 @@
     reciprocal = []
     for q in (0, 1):
         for p in (0, 1):
-            pair_sum = (mu_l[p::2][:, None] + mu_l[q::2][None, :]).reshape(4, 1, 256)
-            reciprocal.append((1.0 / (mu_l[None, :, None] + pair_sum)).reshape(4 * length, 256))
+            pair_sum = (mu_l[p::2][:, None] + mu_l[q::2][None, :]).reshape(1, hl * hl)
+            table = 1.0 / (mu_l[:, None] + pair_sum)
+            reciprocal.append(table.reshape(length, 4, 256).transpose(1, 0, 2).reshape(-1, 256))
     for p, q in CLASSES:
         pair_sum = (mu_n[p::2][:, None] + mu_n[q::2][None, :]).reshape(1, 256)
         reciprocal.append((2.0 / (n + 1)) ** 3 / (mu_n[:, None] + pair_sum))
@@ -255,20 +257,19 @@
     reciprocal.append(ends)
 
     scale = (2.0 / (length + 1)) ** 3
-    flat = np.zeros((32, length))
-    flat[:4] = fine[picks] @ a_full * scale
-    flat[16:] = bm @ a_full * scale
+    blank = np.zeros((12, length))
     lefts = {
         "sl": s_l[:, W : W + n],
-        "source": np.concatenate([a_full, second @ a_full], axis=1) * scale,
-        "flat": flat,
-        "picks": np.concatenate([s_l[picks] * scale, np.zeros((12, length))]),
-        "coefs": b_full * scale,
+        "means": a_full * scale,
+        "flat": np.concatenate([fine[picks], blank[:, :blocks], bm]),
+        "picks": np.concatenate([s_l[picks], blank, b_full]) * scale,
         "sn": s_n,
         "u12": u12,
         "sb": sb,
     }
-    big.update(lefts)
+    for name, value in lefts.items():
+        high, low = split(value)
+        plain[name] = np.concatenate([high, high, low], axis=1)
     singles = {
         "mine": np.stack(mine).astype(np.float32),
         "recip": np.concatenate(reciprocal).astype(np.float32),
@@ -283,11 +284,9 @@
                 parts = split(big[name])
             depth, width = parts[0].shape[-2:]
             place = {"left": (row, depth, width)}
-            lefty = name in lefts
-            step = 256 if not lefty else width
+            step = 256
             tiles = []
             for part in parts:
-                start = row
                 for at in range(0, width, step):
                     tile = np.zeros(part.shape[:-1] + (256,), ml_dtypes.bfloat16)
                     piece = part[..., at : at + step]
@@ -308,10 +307,10 @@
 GROUPS = {
     "first": ["fold", "sl"],
     "upy": ["fy0", "fy1"],
-    "upz": ["fz0", "gz0", "fz1", "gz1", "bz0", "bz1"],
-    "downy": ["by0", "by1", "source"],
+    "upz": ["fz0", "gz0", "fz1", "gz1", "means", "bz0", "bz1"],
+    "downy": ["by0", "by1"],
     "spread": ["spread"],
-    "side": ["flat", "picks", "coefs", "sn", "sb", "u12", "lin"]
+    "side": ["picks", "flat", "sn", "sb", "u12", "lin", "cy0", "cy1"]
     + ["near%d" % c for c in range(4)]
     + ["facex", "facey"],
     "drop": ["drop"],
@@ -339,7 +338,7 @@
     out_ref = refs[count]
     vmem = dict(zip(NAMES, refs[count + 1 : 2 * count + 1]))
     (
-        fold_ref, w_ref, z_ref, b_ref, y_ref,
+        fold_ref, w_ref, z_ref, x_ref, s_ref, b_ref, y_ref, c_ref, d_ref,
         mom_ref, far_ref, near_ref, cx_ref, cy_ref, rx_ref, ry_ref, tally_ref,
         load_sem, f_send, f_recv, p_send, p_recv,
     ) = refs[2 * count + 1 :]
@@ -352,7 +351,16 @@
     modes = near_ref.shape[-1]
 
     loads = {}
-    for i, name in enumerate(NAMES):
+    slabs = []
+    for i in range(4):
+        rows = pl.ds(i * (n // 4), n // 4)
+        slabs.append(
+            pltpu.make_async_copy(
+                hbm["charge"].at[rows], vmem["charge"].at[rows], load_sem.at[len(NAMES) + i - 1]
+            )
+        )
+        slabs[-1].start()
+    for i, name in enumerate(NAMES[1:]):
         source = hbm[name]
         if name in ("spread", "drop"):
             source = source.at[b]
@@ -390,12 +398,12 @@
     def left_mul(name, high, low):
         group, place = places[name]
         row, rows, cols = place["left"]
-        both = mm(vmem[group][row : row + 2 * rows, 0:cols], high)
-        return both[:rows] + both[rows:] + mm(vmem[group][row : row + rows, 0:cols], low)
+        return mm(vmem[group][row : row + rows, 0:cols], jnp.concatenate([high, low, high], axis=0))
 
     groups = [[0, 1, 7, 6], [2, 3, 5, 4]]
     with jax.named_scope("w_charge"):
-        loads["charge"].wait()
+        for slab in slabs:
+            slab.wait()
     with jax.named_scope("w_first"):
         loads["first"].wait()
     with jax.named_scope("fold"):
@@ -418,73 +426,101 @@
         folded = halves(jnp.concatenate(folded, axis=1))
         fold_ref[0] = folded[0]
         fold_ref[1] = folded[1]
-        wide = halves(left_mul("sl", *folded))
         for c in range(4):
             at = slice(c * 256, (c + 1) * 256)
             q = c % 2
-            w_ref[c // 2, q * half : (q + 1) * half] = wide[0][:, at]
-            w_ref[c // 2, (2 + q) * half : (3 + q) * half] = wide[1][:, at]
+            w_ref[c // 2, q * n : (q + 1) * n] = folded[0][:, at]
+            w_ref[c // 2, (2 + q) * n : (3 + q) * n] = folded[1][:, at]
     with jax.named_scope("w_upy"):
         loads["upy"].wait()
     with jax.named_scope("upy"):
         for p in range(2):
             name = "fy%d" % p
             both = mm(w_ref[p], table(name, 0))
-            lift = both[: 2 * half] + both[2 * half :] + mm(w_ref[p, 0 : 2 * half], table(name, 1))
+            lift = both[: 2 * n] + both[2 * n :] + mm(w_ref[p, 0 : 2 * n], table(name, 1))
             high, low = halves(lift)
             for q in range(2):
                 for k in range(4):
-                    at = (4 * p + k) * half
-                    rows, lanes = slice(q * half, (q + 1) * half), slice(k * 128, (k + 1) * 128)
-                    z_ref[q, at : at + half, 0:128] = high[rows, lanes]
-                    z_ref[q, at : at + half, 128:256] = low[rows, lanes]
+                    at = (4 * p + k) * n
+                    rows, lanes = slice(q * n, (q + 1) * n), slice(k * 128, (k + 1) * 128)
+                    z_ref[q, at : at + n, 0:128] = high[rows, lanes]
+                    z_ref[q, at : at + n, 128:256] = low[rows, lanes]
     with jax.named_scope("w_upz"):
         loads["upz"].wait()
-        loads["recip"].wait()
     with jax.named_scope("upz"):
-        rows = 8 * half
         for q in range(2):
             up = mm(z_ref[q], tile("fz%d" % q, 0, 0)) + mm(z_ref[q, :, 0:128], tile("gz%d" % q, 0, 0))
-            high, low = halves(up * vmem["recip"][q * rows : (q + 1) * rows])
-            b_ref[q, 0:rows] = high
-            b_ref[q, rows : 2 * rows] = low
-    with jax.named_scope("downz"):
+            high, low = halves(up)
+            for k in range(8):
+                rows, lanes = slice(k * n, (k + 1) * n), slice((8 * q + k) * 256, (8 * q + k + 1) * 256)
+                x_ref[0:n, lanes] = high[rows]
+                x_ref[n : 2 * n, lanes] = low[rows]
+    with jax.named_scope("w_recip"):
+        loads["recip"].wait()
+    with jax.named_scope("upx"):
+        group, place = places["sl"]
+        row, rows, cols = place["left"]
+        weights = vmem[group][row : row + rows, 0:cols]
+        for q in range(2):
+            lanes = slice(q * 2048, (q + 1) * 2048)
+            spectrum = mm(
+                weights, jnp.concatenate([x_ref[:, lanes], x_ref[0:n, lanes]], axis=0)
+            )
+            divisor = [
+                vmem["recip"][(8 * q + k) * half : (8 * q + k + 1) * half] for k in range(8)
+            ]
+            high, low = halves(spectrum * jnp.concatenate(divisor, axis=1))
+            s_ref[0:half, lanes] = high
+            s_ref[half : 2 * half, lanes] = low
+
+    def down(name, rows, b_ref, y_ref, finish):
+        group, place = places[name]
+        row, _, cols = place["left"]
+        weights = vmem[group][row : row + rows, 0:cols]
+        for q in range(2):
+            lanes = slice(q * 2048, (q + 1) * 2048)
+            short = mm(weights, jnp.concatenate([s_ref[:, lanes], s_ref[0:half, lanes]], axis=0))
+            high, low = halves(short)
+            for k in range(8):
+                lanes = slice(k * 256, (k + 1) * 256)
+                b_ref[q, k * rows : (k + 1) * rows] = high[:, lanes]
+                b_ref[q, (8 + k) * rows : (9 + k) * rows] = low[:, lanes]
         for q in range(2):
             both = mm(b_ref[q], tile("bz%d" % q, 0, 0))
-            high, low = halves(both[:rows, :128] + both[rows:, :128] + both[:rows, 128:])
+            block = 8 * rows
+            high, low = halves(both[:block, :128] + both[block:, :128] + both[:block, 128:])
             for p in range(2):
                 for k in range(4):
-                    at, lanes = (4 * p + k) * half, slice(k * 128, (k + 1) * 128)
-                    y_ref[p, q * half : (q + 1) * half, lanes] = high[at : at + half]
-                    y_ref[p, (2 + q) * half : (3 + q) * half, lanes] = low[at : at + half]
-    with jax.named_scope("w_downy"):
+                    at, lanes = (4 * p + k) * rows, slice(k * 128, (k + 1) * 128)
+                    y_ref[p, q * rows : (q + 1) * rows, lanes] = high[at : at + rows]
+                    y_ref[p, (2 + q) * rows : (3 + q) * rows, lanes] = low[at : at + rows]
+        ys = []
+        finish()
+        for p in range(2):
+            both = mm(y_ref[p], tile("%sy%d" % ("b" if name == "means" else "c", p), 0, 0))
+            both = both[: 2 * rows, :128] + both[2 * rows :, :128] + both[: 2 * rows, 128:]
+            ys += [both[:rows], both[rows:]]
+        return ys
+
+    def arrive():
         loads["downy"].wait()
-    with jax.named_scope("downy"):
-        ys = []
-        for p in range(2):
-            name = "by%d" % p
-            both = mm(y_ref[p], tile(name, 0, 0))
-            both = both[: 2 * half] + both[2 * half :] + mm(y_ref[p, 0 : 2 * half], tile(name, 1, 0))
-            ys += [both[:half], both[half:]]
-        y0, y1, y2, y3 = ys
-    with jax.named_scope("w_spread"):
         loads["spread"].wait()
         loads["mine"].wait()
+
+    with jax.named_scope("down"):
+        y0, y1, y2, y3 = down("means", 16, b_ref, y_ref, arrive)
     with jax.named_scope("spread"):
-        sample = halves(
-            jnp.concatenate(
-                [jnp.where(lane < 64, u[:, :128], v[:, :128]) for u, v in ((y0, y1), (y2, y3))],
-                axis=1,
-            )
-        )
-        high, low = halves(right_mul(*sample, "spread"))
-        packet = left_mul(
-            "source",
-            jnp.concatenate([high[:, :modes], high[:, modes:]], axis=0),
-            jnp.concatenate([low[:, :modes], low[:, modes:]], axis=0),
-        )
+        sample = jnp.concatenate(
+            [jnp.where(lane[0:16] < 64, u, v) for u, v in ((y0, y1), (y2, y3))], axis=1
+        )
+        sample = halves(sample)
+        spread = right_mul(*sample, "spread")
+        bend = spread[:, modes:]
+        gap = jnp.zeros((1, modes), jnp.float32)
+        packet = spread[:, :modes] + 2.0 * bend
+        packet = packet - jnp.concatenate([gap, bend[:-1]]) - jnp.concatenate([bend[1:], gap])
+        mine = vmem["mine"]
         near_ref[n_gy + b] = packet
-        mine = vmem["mine"]
         rightward = jnp.sum(packet * mine[0:16], axis=0, keepdims=True)
         leftward = jnp.sum(packet * mine[16:32], axis=0, keepdims=True)
         for g in range(modes // 128):
@@ -543,23 +579,18 @@
     with jax.named_scope("w_side"):
         loads["side"].wait()
     with jax.named_scope("lin"):
-        coef = halves(jnp.concatenate([u[:, 128:] for u in (y0, y1, y2, y3)], axis=1))
-        slab = halves(jnp.where(lane < 32, y0[:, 128:] + y2[:, 128:], y1[:, 128:] + y3[:, 128:]))
+        y0, y1, y2, y3 = down("picks", 32, c_ref, d_ref, lambda: None)
         flat = right_mul(*halves(left_mul("flat", *sample)), "lin")
-        coef = left_mul("picks", *coef)[0:8]
         cx = jnp.concatenate(
             [
-                jnp.where(
-                    lane[0:8] < 64,
-                    pltpu.roll(coef[:, c * 128 : (c + 1) * 128], 64, 1),
-                    coef[:, (c + 1) * 128 : (c + 2) * 128],
-                )
-                for c in (0, 2)
+                jnp.where(lane[0:8] < 64, pltpu.roll(u[0:8], 64, 1), v[0:8])
+                for u, v in ((y0, y1), (y2, y3))
             ],
             axis=1,
         )
         cx = cx - flat[0:8, 0:256]
-        cy = left_mul("coefs", *slab) - flat[16:32, 256:384]
+        cy = jnp.where(lane[0:16] < 32, y0[16:] + y2[16:], y1[16:] + y3[16:])
+        cy = cy - flat[16:32, 256:384]
         cx_ref[...] = cx
         cy_ref[...] = cy
 
@@ -721,10 +752,14 @@
     half = P_SIZE + 2 * W
     scratch += [
         pltpu.VMEM((2, P_SIZE, 1024), jnp.bfloat16),
-        pltpu.VMEM((2, 4 * half, 256), jnp.bfloat16),
-        pltpu.VMEM((2, 8 * half, 256), jnp.bfloat16),
-        pltpu.VMEM((2, 16 * half, 256), jnp.bfloat16),
-        pltpu.VMEM((2, 4 * half, 512), jnp.bfloat16),
+        pltpu.VMEM((2, 4 * P_SIZE, 256), jnp.bfloat16),
+        pltpu.VMEM((2, 8 * P_SIZE, 256), jnp.bfloat16),
+        pltpu.VMEM((2 * P_SIZE, 4096), jnp.bfloat16),
+        pltpu.VMEM((2 * half, 4096), jnp.bfloat16),
+        pltpu.VMEM((2, 256, 256), jnp.bfloat16),
+        pltpu.VMEM((2, 64, 512), jnp.bfloat16),
+        pltpu.VMEM((2, 512, 256), jnp.bfloat16),
+        pltpu.VMEM((2, 128, 512), jnp.bfloat16),
         pltpu.VMEM((modes // 128, 8, 128), jnp.float32),
         pltpu.VMEM((n_gy, modes // 128, n_gx, 128), jnp.float32),
         pltpu.VMEM((3 * n_gy, 16, modes), jnp.float32),
@@ -733,7 +768,7 @@
         pltpu.VMEM((8, 256), jnp.float32),
         pltpu.VMEM((2, 16, 128), jnp.float32),
         pltpu.VMEM((16 * (modes // 128) * (3 * n_gy - 1) + 40, 128), jnp.float32),
-        pltpu.SemaphoreType.DMA((len(NAMES),)),
+        pltpu.SemaphoreType.DMA((len(NAMES) + 3,)),
         pltpu.SemaphoreType.DMA,
         pltpu.SemaphoreType.DMA,
         pltpu.SemaphoreType.DMA,

time: 13.7 us -> 13.4 us (0.978)
  Pallas kernels: 13.6 us -> 13.3 us
    pallas_call x1, Pallas kernels: 12.9 us -> 12.6 us  [body(): pl.pallas_call(functools.partial(kernel, places, n_gx, n_gy), out_shape=p...]
where the time goes in v4:
time: 13.4 us; the launch traced here: 13.3 us
  Pallas kernels  13.3 us (99%)
    pallas_call x1, Pallas kernels, body(): pl.pallas_call(functools.partial(kernel, places, n_gx, n_gy), out_shape=p...  12.6 us
    pallas_call x1, Pallas kernels, body(): pl.pallas_call(emit, out_shape=jax.ShapeDtypeStruct(charge.shape, charge....  0.67 us

profile of v4, /device:TPU:0, one launch (start us, length us, event | category | flops | bytes accessed | tf_op | source)
XLA Modules:
  0.0 13.3 jit_solution(605319499664151156)
XLA Ops:
  0.0 12.6 %mlc.1.in_ref = f32[32,1024]{1,0:T(8,128)S(1)} custom-call(f32[32,1024]{1,0:T(8,128)} %refs_0_.1, bf16[320,256]{1,0:T(8,128)(2,1)} %constant.20.clone.refs_1_, bf16[2048,256]{1,0:T(8,128)(2,1)} %constant.21.clone.refs_2_, bf16[1296,256]{1,0:T(8,128)(2,1)} %constant.22.clone.refs_3_, f32[1184,256]{1,0:T(8,128)} %constant.23.clone.refs_4_, ...), custom_call_target="tpu_custom_call" | custom-call | tf_op jit(solution)/shard_map/mlc/pallas_call | solution.py:779
  12.6 0.7 %emit.1 = f32[32,1024]{1,0:T(8,128)} custom-call(f32[32,1024]{1,0:T(8,128)S(1)} %mlc.1.in_ref), custom_call_target="tpu_custom_call" | custom-call | tf_op jit(solution)/shard_map/emit/pallas_call | solution.py:790

commit v5 on v4

--- a/solution.py
+++ b/solution.py
@@ -85,13 +85,6 @@
     order = np.arange(4 * NL).reshape(4, hn, 2).transpose(2, 0, 1).ravel()
     big = {}
 
-    folding = np.zeros((2, 4, n, 2, 2, 4, half))
-    for p, q in CLASSES:
-        for y4 in range(4):
-            piece = u_n[q * half : (q + 1) * half].T
-            folding[0, y4, :, p, q, y4, :] = piece
-            folding[1, y4, :, p, q, 3 - y4, :] = piece if p == 0 else -piece
-    plain = {"fold": folding.reshape(256, 256)}
     folding = np.zeros((4, 4, n, 4, 2 * 4, half))
     for c, (p, q) in enumerate(CLASSES):
         for vi in range(4):
@@ -100,7 +93,7 @@
                 sign = -1.0 if vi > 1 and p == 1 else 1.0
                 folding[vi, y4, :, c, il, :] = sign * u_n[q * half : (q + 1) * half].T
     folding = folding.reshape(4 * 128, 4 * 128)
-    plain["unfold"] = folding.T
+    plain = {"unfold": folding.T}
 
     inner = s_l[:, W : W + n] @ u_n.T / 2
     f1 = [inner[p::2, p * half : (p + 1) * half] for p in (0, 1)]
@@ -108,8 +101,10 @@
     b1 = [b_full[p::2, p::2] for p in (0, 1)]
     keep, pick = np.eye(hb), np.concatenate([np.zeros((hn, hb)), np.eye(hn)], axis=1)
     keep = np.concatenate([keep, np.zeros((hb, hn))], axis=1)
+    compact = []
     for p in (0, 1):
-        big["fy%d" % p] = np.kron(f1[p].T, np.eye(half))
+        for part in split(np.repeat(f1[p].T, half, axis=1)):
+            compact.append(part.astype(np.float32))
         high, low = split(np.kron(np.eye(8), f1[p].T))
         plain["fz%d" % p] = np.concatenate([high, high])
         plain["gz%d" % p] = low
@@ -273,6 +268,7 @@
     singles = {
         "mine": np.stack(mine).astype(np.float32),
         "recip": np.concatenate(reciprocal).astype(np.float32),
+        "compact": np.concatenate(compact),
     }
     places = {}
     for group, names in GROUPS.items():
@@ -305,9 +301,7 @@
 
 
 GROUPS = {
-    "first": ["fold", "sl"],
-    "upy": ["fy0", "fy1"],
-    "upz": ["fz0", "gz0", "fz1", "gz1", "means", "bz0", "bz1"],
+    "upz": ["fz0", "gz0", "fz1", "gz1", "sl", "means", "bz0", "bz1"],
     "downy": ["by0", "by1"],
     "spread": ["spread"],
     "side": ["picks", "flat", "sn", "sb", "u12", "lin", "cy0", "cy1"]
@@ -316,7 +310,14 @@
     "drop": ["drop"],
     "last": ["far%d" % c for c in range(4)] + ["unfold"],
 }
-NAMES = ["charge", "first", "upy", "upz", "recip", "downy", "spread", "mine", "side", "drop", "last"]
+NAMES = [
+    "charge", "compact", "upz", "recip", "downy", "spread", "mine", "side", "drop", "last",
+]
+WAITS = [
+    ["charge"], ["compact"], ["upz"], ["recip"], ["downy", "spread"], ["mine"],
+    ["side", "drop", "last"],
+]
+CUTS = {"charge": 4, "compact": 4}
 
 
 def halves(value):
@@ -336,12 +337,13 @@
     count = len(NAMES)
     hbm = dict(zip(NAMES, refs[:count]))
     out_ref = refs[count]
-    vmem = dict(zip(NAMES, refs[count + 1 : 2 * count + 1]))
+    charge_ref, compact_ref, recip_ref, mine_ref, tables_ref = refs[count + 1 : count + 6]
+    vmem = {"charge": charge_ref, "compact": compact_ref, "recip": recip_ref, "mine": mine_ref}
     (
-        fold_ref, w_ref, z_ref, x_ref, s_ref, b_ref, y_ref, c_ref, d_ref,
+        sign_ref, grow_ref, fold_ref, w_ref, z_ref, x_ref, s_ref, b_ref, y_ref, c_ref, d_ref,
         mom_ref, far_ref, near_ref, cx_ref, cy_ref, rx_ref, ry_ref, tally_ref,
         load_sem, f_send, f_recv, p_send, p_recv,
-    ) = refs[2 * count + 1 :]
+    ) = refs[count + 6 :]
     ndev = n_gx * n_gy
     a = lax.axis_index("gx")
     b = lax.axis_index("gy")
@@ -350,24 +352,28 @@
     half = n + 2 * W
     modes = near_ref.shape[-1]
 
-    loads = {}
-    slabs = []
-    for i in range(4):
-        rows = pl.ds(i * (n // 4), n // 4)
-        slabs.append(
-            pltpu.make_async_copy(
-                hbm["charge"].at[rows], vmem["charge"].at[rows], load_sem.at[len(NAMES) + i - 1]
-            )
-        )
-        slabs[-1].start()
-    for i, name in enumerate(NAMES[1:]):
-        source = hbm[name]
-        if name in ("spread", "drop"):
-            source = source.at[b]
-        if name == "mine":
-            source = source.at[a]
-        loads[name] = pltpu.make_async_copy(source, vmem[name], load_sem.at[i])
-        loads[name].start()
+    loads, base = {}, 0
+    for i, names in enumerate(WAITS):
+        start = base
+        for name in names:
+            source = hbm[name]
+            if name in ("spread", "drop"):
+                source = source.at[b]
+            if name == "mine":
+                source = source.at[a]
+            if name in GROUPS:
+                rows = source.shape[0]
+                vmem[name] = tables_ref.at[pl.ds(base, rows)]
+                base += rows
+            cuts = CUTS.get(name, 1)
+            each = source.shape[0] // cuts
+            for k in range(cuts):
+                part = pl.ds(k * each, each)
+                pltpu.make_async_copy(
+                    source.at[part], vmem[name].at[part], load_sem.at[i]
+                ).start()
+        target = tables_ref.at[pl.ds(start, base - start)] if base > start else vmem[names[0]]
+        loads[names[0]] = pltpu.make_async_copy(target, target, load_sem.at[i])
 
     barrier = pltpu.get_barrier_semaphore()
 
@@ -401,11 +407,20 @@
         return mm(vmem[group][row : row + rows, 0:cols], jnp.concatenate([high, low, high], axis=0))
 
     groups = [[0, 1, 7, 6], [2, 3, 5, 4]]
+    with jax.named_scope("signs"):
+        z = lax.broadcasted_iota(jnp.int32, (n, 256), 0)
+        at = lax.broadcasted_iota(jnp.int32, (n, 256), 1)
+        odd = jnp.where((at // 64) % 2 == 1, -1.0, 1.0)
+        base = jnp.where(z == at % 16, 1.0, 0.0) + jnp.where(z == 31 - at % 16, odd, 0.0)
+        for side in range(2):
+            for y in range(4):
+                spot = (at // 16) % 4 == (3 - y if side else y)
+                flip = jnp.where(at >= 128, -1.0, 1.0) if side else 1.0
+                rows = (side * 4 + y) * n
+                sign_ref[rows : rows + n] = jnp.where(spot, base * flip, 0.0).astype(jnp.bfloat16)
+
     with jax.named_scope("w_charge"):
-        for slab in slabs:
-            slab.wait()
-    with jax.named_scope("w_first"):
-        loads["first"].wait()
+        loads["charge"].wait()
     with jax.named_scope("fold"):
         charge = vmem["charge"]
         pairs = [
@@ -413,7 +428,7 @@
             for u in range(4)
         ]
         high, low = halves(jnp.concatenate(pairs, axis=0))
-        both = mm(jnp.concatenate([high, low], axis=0), tile("fold", 0, 0))
+        both = mm(jnp.concatenate([high, low], axis=0), sign_ref[...])
         both = both[: 4 * n] + both[4 * n :]
         lane = lax.broadcasted_iota(jnp.int32, (half, 128), 1)
         folded = []
@@ -431,13 +446,19 @@
             q = c % 2
             w_ref[c // 2, q * n : (q + 1) * n] = folded[0][:, at]
             w_ref[c // 2, (2 + q) * n : (3 + q) * n] = folded[1][:, at]
-    with jax.named_scope("w_upy"):
-        loads["upy"].wait()
+    with jax.named_scope("grow"):
+        loads["compact"].wait()
+        same = lax.broadcasted_iota(jnp.int32, (16, 512), 0)
+        same = jnp.where(lax.broadcasted_iota(jnp.int32, (16, 512), 1) % 16 == same, 1.0, 0.0)
+        same = same.astype(jnp.bfloat16)
+        for t in range(4):
+            for i in range(16):
+                line = jnp.broadcast_to(compact_ref[t * 16 + i : t * 16 + i + 1], (16, 512))
+                grow_ref[t, i * 16 : (i + 1) * 16] = line.astype(jnp.bfloat16) * same
     with jax.named_scope("upy"):
         for p in range(2):
-            name = "fy%d" % p
-            both = mm(w_ref[p], table(name, 0))
-            lift = both[: 2 * n] + both[2 * n :] + mm(w_ref[p, 0 : 2 * n], table(name, 1))
+            both = mm(w_ref[p], grow_ref[2 * p])
+            lift = both[: 2 * n] + both[2 * n :] + mm(w_ref[p, 0 : 2 * n], grow_ref[2 * p + 1])
             high, low = halves(lift)
             for q in range(2):
                 for k in range(4):
@@ -504,7 +525,6 @@
 
     def arrive():
         loads["downy"].wait()
-        loads["spread"].wait()
         loads["mine"].wait()
 
     with jax.named_scope("down"):
@@ -680,10 +700,6 @@
             values.append(jnp.sum(influence * source, axis=0, keepdims=True))
         values.append(jnp.zeros((16 - len(values), modes), jnp.float32))
         lifted = left_mul("u12", *halves(jnp.concatenate(values, axis=0)))
-
-    with jax.named_scope("w_last"):
-        loads["drop"].wait()
-        loads["last"].wait()
 
     def settle_far(each):
         block = far_ref.at[:, :, pl.ds(0, each)]
@@ -745,12 +761,15 @@
 def body(n_gx, n_gy, charge):
     singles, places = tables(n_gx, n_gy)
     arrays = [charge] + [jnp.asarray(singles[name]) for name in NAMES[1:]]
-    scratch = [
-        pltpu.VMEM(window(name, array.shape), array.dtype) for name, array in zip(NAMES, arrays)
-    ]
+    shapes = {name: window(name, array.shape) for name, array in zip(NAMES, arrays)}
+    total = sum(shapes[name][0] for name in GROUPS)
+    scratch = [pltpu.VMEM(shapes[name], jnp.float32) for name in ("charge", "compact", "recip", "mine")]
+    scratch.append(pltpu.VMEM((total, 256), jnp.bfloat16))
     modes = n_gy * (P_SIZE // Q) ** 2
     half = P_SIZE + 2 * W
     scratch += [
+        pltpu.VMEM((256, 256), jnp.bfloat16),
+        pltpu.VMEM((4, 256, 512), jnp.bfloat16),
         pltpu.VMEM((2, P_SIZE, 1024), jnp.bfloat16),
         pltpu.VMEM((2, 4 * P_SIZE, 256), jnp.bfloat16),
         pltpu.VMEM((2, 8 * P_SIZE, 256), jnp.bfloat16),
@@ -768,7 +787,7 @@
         pltpu.VMEM((8, 256), jnp.float32),
         pltpu.VMEM((2, 16, 128), jnp.float32),
         pltpu.VMEM((16 * (modes // 128) * (3 * n_gy - 1) + 40, 128), jnp.float32),
-        pltpu.SemaphoreType.DMA((len(NAMES) + 3,)),
+        pltpu.SemaphoreType.DMA((len(WAITS),)),
         pltpu.SemaphoreType.DMA,
         pltpu.SemaphoreType.DMA,
         pltpu.SemaphoreType.DMA,

time: 13.4 us -> 13.1 us (0.978)
  Pallas kernels: 13.3 us -> 12.9 us
    pallas_call x1, Pallas kernels: 12.6 us -> 12.3 us  [body(): pl.pallas_call(functools.partial(kernel, places, n_gx, n_gy), out_shape=p...]
where the time goes in v5:
time: 13.1 us; the launch traced here: 12.9 us
  Pallas kernels  12.9 us (98%)
    pallas_call x1, Pallas kernels, body(): pl.pallas_call(functools.partial(kernel, places, n_gx, n_gy), out_shape=p...  12.3 us
    pallas_call x1, Pallas kernels, body(): pl.pallas_call(emit, out_shape=jax.ShapeDtypeStruct(charge.shape, charge....  0.67 us

profile of v5, /device:TPU:0, one launch (start us, length us, event | category | flops | bytes accessed | tf_op | source)
XLA Modules:
  0.0 12.9 jit_solution(10558823636624588515)
XLA Ops:
  0.0 12.3 %mlc.1.in_ref = f32[32,1024]{1,0:T(8,128)S(1)} custom-call(f32[32,1024]{1,0:T(8,128)} %refs_0_.1, f32[64,512]{1,0:T(8,128)} %constant.18.clone.refs_1_, bf16[1360,256]{1,0:T(8,128)(2,1)} %constant.19.clone.refs_2_, f32[1184,256]{1,0:T(8,128)} %constant.20.clone.refs_3_, bf16[1024,256]{1,0:T(8,128)(2,1)} %constant.21.clone.refs_4_, ...), custom_call_target="tpu_custom_call" | custom-call | tf_op jit(solution)/shard_map/mlc/pallas_call | solution.py:798
  12.3 0.7 %emit.1 = f32[32,1024]{1,0:T(8,128)} custom-call(f32[32,1024]{1,0:T(8,128)S(1)} %mlc.1.in_ref), custom_call_target="tpu_custom_call" | custom-call | tf_op jit(solution)/shard_map/emit/pallas_call | solution.py:809

commit v6 on v5

--- a/solution.py
+++ b/solution.py
@@ -408,44 +408,38 @@
 
     groups = [[0, 1, 7, 6], [2, 3, 5, 4]]
     with jax.named_scope("signs"):
-        z = lax.broadcasted_iota(jnp.int32, (n, 256), 0)
-        at = lax.broadcasted_iota(jnp.int32, (n, 256), 1)
-        odd = jnp.where((at // 64) % 2 == 1, -1.0, 1.0)
+        z = lax.broadcasted_iota(jnp.int32, (n, 512), 0)
+        at = lax.broadcasted_iota(jnp.int32, (n, 512), 1)
+        odd = jnp.where((at // 128) % 2 == 1, -1.0, 1.0)
         base = jnp.where(z == at % 16, 1.0, 0.0) + jnp.where(z == 31 - at % 16, odd, 0.0)
-        for side in range(2):
-            for y in range(4):
-                spot = (at // 16) % 4 == (3 - y if side else y)
-                flip = jnp.where(at >= 128, -1.0, 1.0) if side else 1.0
-                rows = (side * 4 + y) * n
-                sign_ref[rows : rows + n] = jnp.where(spot, base * flip, 0.0).astype(jnp.bfloat16)
+        turned = jnp.where(at >= 256, -base, base)
+        spot = (at // 16) % 8
+        for side, value in ((0, base), (1, turned)):
+            for y in range(8):
+                rows = (side * 8 + y) * n
+                match = spot == ((3 - y) % 8 if side else y)
+                sign_ref[rows : rows + n] = jnp.where(match, value, 0.0).astype(jnp.bfloat16)
 
     with jax.named_scope("w_charge"):
         loads["charge"].wait()
     with jax.named_scope("fold"):
         charge = vmem["charge"]
-        pairs = [
-            jnp.concatenate([charge[:, v * 128 : (v + 1) * 128] for v in (u, 7 - u)], axis=1)
-            for u in range(4)
+        sides = [
+            jnp.concatenate([charge[:, v * 128 : (v + 1) * 128] for v in group], axis=1)
+            for group in groups
         ]
-        high, low = halves(jnp.concatenate(pairs, axis=0))
+        high, low = halves(jnp.concatenate(sides, axis=0))
         both = mm(jnp.concatenate([high, low], axis=0), sign_ref[...])
-        both = both[: 4 * n] + both[4 * n :]
+        parts = halves(both[: 2 * n] + both[2 * n :])
         lane = lax.broadcasted_iota(jnp.int32, (half, 128), 1)
-        folded = []
-        for p in range(2):
-            rows = [both[v * n : (v + 1) * n, p * 128 : (p + 1) * 128] for v in range(4)]
-            turn = [pltpu.roll(row, 64, 1) for row in rows]
-            left = lane[:n] < 64
-            folded += [jnp.where(left, rows[v], turn[v + 1]) for v in (0, 2)]
-            folded += [jnp.where(left, turn[v], rows[v + 1]) for v in (0, 2)]
-        folded = halves(jnp.concatenate(folded, axis=1))
-        fold_ref[0] = folded[0]
-        fold_ref[1] = folded[1]
-        for c in range(4):
-            at = slice(c * 256, (c + 1) * 256)
-            q = c % 2
-            w_ref[c // 2, q * n : (q + 1) * n] = folded[0][:, at]
-            w_ref[c // 2, (2 + q) * n : (3 + q) * n] = folded[1][:, at]
+        for k, part in enumerate(parts):
+            for c in range(4):
+                for side in range(2):
+                    piece = part[side * n : (side + 1) * n, c * 128 : (c + 1) * 128]
+                    at = c * 256 + side * 128
+                    fold_ref[k, :, at : at + 128] = piece
+                    rows = (2 * k + c % 2) * n
+                    w_ref[c // 2, rows : rows + n, side * 128 : (side + 1) * 128] = piece
     with jax.named_scope("grow"):
         loads["compact"].wait()
         same = lax.broadcasted_iota(jnp.int32, (16, 512), 0)
@@ -500,7 +494,9 @@
         weights = vmem[group][row : row + rows, 0:cols]
         for q in range(2):
             lanes = slice(q * 2048, (q + 1) * 2048)
-            short = mm(weights, jnp.concatenate([s_ref[:, lanes], s_ref[0:half, lanes]], axis=0))
+            stacked = jnp.concatenate([weights[:, 0:half], weights[:, 2 * half : 3 * half]], axis=0)
+            short = mm(stacked, s_ref[0:half, lanes])
+            short = short[:rows] + short[rows:] + mm(weights[:, 0:half], s_ref[half:, lanes])
             high, low = halves(short)
             for k in range(8):
                 lanes = slice(k * 256, (k + 1) * 256)
@@ -768,7 +764,7 @@
     modes = n_gy * (P_SIZE // Q) ** 2
     half = P_SIZE + 2 * W
     scratch += [
-        pltpu.VMEM((256, 256), jnp.bfloat16),
+        pltpu.VMEM((512, 512), jnp.bfloat16),
         pltpu.VMEM((4, 256, 512), jnp.bfloat16),
         pltpu.VMEM((2, P_SIZE, 1024), jnp.bfloat16),
         pltpu.VMEM((2, 4 * P_SIZE, 256), jnp.bfloat16),

time: 13.1 us -> 13 us (level)
  no operation moved by 1% of the time
where the time goes in v6:
time: 13 us; the launch traced here: 12.9 us
  Pallas kernels  12.9 us (99%)
    pallas_call x1, Pallas kernels, body(): pl.pallas_call(functools.partial(kernel, places, n_gx, n_gy), out_shape=p...  12.2 us
    pallas_call x1, Pallas kernels, body(): pl.pallas_call(emit, out_shape=jax.ShapeDtypeStruct(charge.shape, charge....  0.67 us

profile of v6, /device:TPU:0, one launch (start us, length us, event | category | flops | bytes accessed | tf_op | source)
XLA Modules:
  0.0 12.9 jit_solution(7353748170317317451)
XLA Ops:
  0.0 12.2 %mlc.1.in_ref = f32[32,1024]{1,0:T(8,128)S(1)} custom-call(f32[32,1024]{1,0:T(8,128)} %refs_0_.1, f32[64,512]{1,0:T(8,128)} %constant.18.clone.refs_1_, bf16[1360,256]{1,0:T(8,128)(2,1)} %constant.19.clone.refs_2_, f32[1184,256]{1,0:T(8,128)} %constant.20.clone.refs_3_, bf16[1024,256]{1,0:T(8,128)(2,1)} %constant.21.clone.refs_4_, ...), custom_call_target="tpu_custom_call" | custom-call | tf_op jit(solution)/shard_map/mlc/pallas_call | solution.py:794
  12.2 0.7 %emit.1 = f32[32,1024]{1,0:T(8,128)} custom-call(f32[32,1024]{1,0:T(8,128)S(1)} %mlc.1.in_ref), custom_call_target="tpu_custom_call" | custom-call | tf_op jit(solution)/shard_map/emit/pallas_call | solution.py:805

commit v7 on v6

--- a/solution.py
+++ b/solution.py
@@ -340,7 +340,7 @@
     charge_ref, compact_ref, recip_ref, mine_ref, tables_ref = refs[count + 1 : count + 6]
     vmem = {"charge": charge_ref, "compact": compact_ref, "recip": recip_ref, "mine": mine_ref}
     (
-        sign_ref, grow_ref, fold_ref, w_ref, z_ref, x_ref, s_ref, b_ref, y_ref, c_ref, d_ref,
+        sign_ref, grow_ref, sample_ref, spec_ref, fold_ref, w_ref, z_ref, x_ref, s_ref, b_ref, y_ref, c_ref, d_ref,
         mom_ref, far_ref, near_ref, cx_ref, cy_ref, rx_ref, ry_ref, tally_ref,
         load_sem, f_send, f_recv, p_send, p_recv,
     ) = refs[count + 6 :]
@@ -530,6 +530,8 @@
             [jnp.where(lane[0:16] < 64, u, v) for u, v in ((y0, y1), (y2, y3))], axis=1
         )
         sample = halves(sample)
+        sample_ref[0] = sample[0]
+        sample_ref[1] = sample[1]
         spread = right_mul(*sample, "spread")
         bend = spread[:, modes:]
         gap = jnp.zeros((1, modes), jnp.float32)
@@ -543,9 +545,6 @@
             mom_ref[g, 0:1] = rightward[:, g * 128 : (g + 1) * 128]
             mom_ref[g, 1:2] = leftward[:, g * 128 : (g + 1) * 128]
 
-    with jax.named_scope("barrier"):
-        pl.semaphore_wait(barrier, ndev - 1)
-
     def remote(source, target, send, recv, device):
         return pltpu.make_async_remote_copy(
             src_ref=source,
@@ -573,68 +572,103 @@
 
         return carry
 
-    with jax.named_scope("send"):
-        lax.fori_loop(1, n_gx - 1, start_far, 0)
-        for step in (0, 1, 2):
-            for j in range(n_gy):
-                other = a + step - 1
-                fine = (other >= 0) & (other < n_gx)
-                if step == 1:
-                    fine = b != j
-
-                @pl.when(fine)
-                def _():
-                    remote(
-                        near_ref.at[n_gy + b],
-                        near_ref.at[(2 - step) * n_gy + b],
-                        p_send,
-                        p_recv,
-                        (other, j),
-                    ).start()
-
-    with jax.named_scope("w_side"):
-        loads["side"].wait()
-    with jax.named_scope("lin"):
-        y0, y1, y2, y3 = down("picks", 32, c_ref, d_ref, lambda: None)
-        flat = right_mul(*halves(left_mul("flat", *sample)), "lin")
-        cx = jnp.concatenate(
-            [
-                jnp.where(lane[0:8] < 64, pltpu.roll(u[0:8], 64, 1), v[0:8])
-                for u, v in ((y0, y1), (y2, y3))
-            ],
-            axis=1,
-        )
-        cx = cx - flat[0:8, 0:256]
-        cy = jnp.where(lane[0:16] < 32, y0[16:] + y2[16:], y1[16:] + y3[16:])
-        cy = cy - flat[16:32, 256:384]
-        cx_ref[...] = cx
-        cy_ref[...] = cy
+    early = a < n_gx // 4
+
+    def send_far():
+        with jax.named_scope("sendf"):
+            lax.fori_loop(1, n_gx - 1, start_far, 0)
+
+    def send_near():
+        with jax.named_scope("send"):
+            for step in (0, 1, 2):
+                for j in range(n_gy):
+                    other = a + step - 1
+                    fine = (other >= 0) & (other < n_gx)
+                    if step == 1:
+                        fine = b != j
+
+                    @pl.when(fine)
+                    def _():
+                        remote(
+                            near_ref.at[n_gy + b],
+                            near_ref.at[(2 - step) * n_gy + b],
+                            p_send,
+                            p_recv,
+                            (other, j),
+                        ).start()
 
     upper, lower = lax.rem(b + 1, n_gy), lax.rem(b + n_gy - 1, n_gy)
-    with jax.named_scope("sendc"):
-
-        @pl.when(a < n_gx - 1)
+    def send_faces():
+        with jax.named_scope("sendc"):
+
+            @pl.when(a < n_gx - 1)
+            def _():
+                remote(
+                    cx_ref.at[pl.ds(2, 1)], rx_ref.at[pl.ds(0, 1)], p_send, p_recv, (a + 1, b)
+                ).start()
+
+            @pl.when(a > 0)
+            def _():
+                remote(
+                    cx_ref.at[pl.ds(1, 1)], rx_ref.at[pl.ds(1, 1)], p_send, p_recv, (a - 1, b)
+                ).start()
+
+            remote(cy_ref, ry_ref.at[0], p_send, p_recv, (a, upper)).start()
+            remote(cy_ref, ry_ref.at[1], p_send, p_recv, (a, lower)).start()
+
+    def turn(step, carry):
+        @pl.when(step == last)
         def _():
-            remote(
-                cx_ref.at[pl.ds(2, 1)], rx_ref.at[pl.ds(0, 1)], p_send, p_recv, (a + 1, b)
-            ).start()
-
-        @pl.when(a > 0)
+            with jax.named_scope("barrier"):
+                pl.semaphore_wait(barrier, ndev - 1)
+
+            @pl.when(early)
+            def _():
+                send_faces()
+                send_near()
+                send_far()
+
+            @pl.when(jnp.logical_not(early))
+            def _():
+                send_far()
+                send_near()
+
+        @pl.when(step != last)
         def _():
-            remote(
-                cx_ref.at[pl.ds(1, 1)], rx_ref.at[pl.ds(1, 1)], p_send, p_recv, (a - 1, b)
-            ).start()
-
-        remote(cy_ref, ry_ref.at[0], p_send, p_recv, (a, upper)).start()
-        remote(cy_ref, ry_ref.at[1], p_send, p_recv, (a, lower)).start()
-
-    with jax.named_scope("near"):
-        narrow = halves(left_mul("sn", fold_ref[0], fold_ref[1]))
-        spectrum = []
-        for c in range(4):
-            at = slice(c * 256, (c + 1) * 256)
-            spectrum.append(right_mul(narrow[0][:, at], narrow[1][:, at], "near%d" % c))
-        spectrum = jnp.concatenate(spectrum, axis=1)
+            with jax.named_scope("w_side"):
+                loads["side"].wait()
+            with jax.named_scope("lin"):
+                y0, y1, y2, y3 = down("picks", 32, c_ref, d_ref, lambda: None)
+                flat = right_mul(*halves(left_mul("flat", sample_ref[0], sample_ref[1])), "lin")
+                cx = jnp.concatenate(
+                    [
+                        jnp.where(lane[0:8] < 64, pltpu.roll(u[0:8], 64, 1), v[0:8])
+                        for u, v in ((y0, y1), (y2, y3))
+                    ],
+                    axis=1,
+                )
+                cx = cx - flat[0:8, 0:256]
+                cy = jnp.where(lane[0:16] < 32, y0[16:] + y2[16:], y1[16:] + y3[16:])
+                cy = cy - flat[16:32, 256:384]
+                cx_ref[...] = cx
+                cy_ref[...] = cy
+
+            with jax.named_scope("near"):
+                narrow = halves(left_mul("sn", fold_ref[0], fold_ref[1]))
+                spectrum = []
+                for c in range(4):
+                    at = slice(c * 256, (c + 1) * 256)
+                    spectrum.append(right_mul(narrow[0][:, at], narrow[1][:, at], "near%d" % c))
+                spec_ref[...] = jnp.concatenate(spectrum, axis=1)
+
+        return carry
+
+    last = jnp.where(early, 1, 0)
+    lax.fori_loop(0, 2, turn, 0)
+
+    @pl.when(jnp.logical_not(early))
+    def _():
+        send_faces()
 
     edge = (a == 0) | (a == n_gx - 1)
     inner = jnp.logical_not(edge)
@@ -655,6 +689,7 @@
             settle_near(2)
 
     with jax.named_scope("face"):
+        cx, cy, spectrum = cx_ref[...], cy_ref[...], spec_ref[...]
         from_left = jnp.where(a > 0, rx_ref[0:1], 0.0)
         from_right = jnp.where(a < n_gx - 1, rx_ref[1:2], 0.0)
         ends = jnp.concatenate(
@@ -697,6 +732,35 @@
         values.append(jnp.zeros((16 - len(values), modes), jnp.float32))
         lifted = left_mul("u12", *halves(jnp.concatenate(values, axis=0)))
 
+    inverse = jnp.concatenate(
+        [vmem["recip"][fine + c * n : fine + (c + 1) * n] for c in range(4)], axis=1
+    )
+
+    def unfolded(parts):
+        sides = [
+            jnp.concatenate([part[:, s * 128 : (s + 1) * 128] for part in parts], axis=1)
+            for s in range(2)
+        ]
+        return jnp.concatenate(sides, axis=0)
+
+    def cells_of(both):
+        for s, group in enumerate(groups):
+            for i, v in enumerate(group):
+                yield v, both[s * n : (s + 1) * n, i * 128 : (i + 1) * 128]
+
+    with jax.named_scope("base"):
+        lifted = halves(jnp.concatenate([lifted[:n], lifted[n:]], axis=1))
+        spectrum = (spectrum + right_mul(*lifted, "drop")) * inverse
+        high, low = halves(left_mul("sn", *halves(spectrum)))
+        parts = []
+        for c in range(4):
+            at = slice(c * 256, (c + 1) * 256)
+            parts.append(right_mul(high[:, at], low[:, at], "far%d" % c))
+        high, low = halves(unfolded(parts))
+        both = mm(jnp.concatenate([high, low], axis=0), table("unfold", 0))
+        for v, value in cells_of(both[: 2 * n] + both[2 * n :]):
+            out_ref[:, v * 128 : (v + 1) * 128] = value
+
     def settle_far(each):
         block = far_ref.at[:, :, pl.ds(0, each)]
         remote(block, block, f_send, f_recv, (a, b)).wait()
@@ -721,31 +785,18 @@
             after = after + jnp.where(origin >= a + 2, sent, 0.0)
         before = jnp.sum(before * mine[256 : 256 + n_gx], axis=0, keepdims=True)
         after = jnp.sum(after * mine[256 + n_gx : 256 + 2 * n_gx], axis=0, keepdims=True)
-        lifted = lifted + mine[32:96] * before + mine[96:160] * after
-        lifted = halves(jnp.concatenate([lifted[:n], lifted[n:]], axis=1))
-        inverse = jnp.concatenate(
-            [vmem["recip"][fine + c * n : fine + (c + 1) * n] for c in range(4)], axis=1
-        )
-        spectrum = (spectrum + right_mul(*lifted, "drop")) * inverse
-        high, low = halves(left_mul("sn", *halves(spectrum)))
-        parts = []
-        for c in range(4):
-            at = slice(c * 256, (c + 1) * 256)
-            parts.append(right_mul(high[:, at], low[:, at], "far%d" % c))
+        lifted = mine[32:96] * before + mine[96:160] * after
+        lifted = jnp.concatenate([lifted[:n], lifted[n:]], axis=1).astype(jnp.bfloat16)
+        spectrum = (mm(lifted, table("drop", 0)) * inverse).astype(jnp.bfloat16)
+        group, place = places["sn"]
+        row, rows, _ = place["left"]
+        spectrum = mm(vmem[group][row : row + rows, 0:n], spectrum).astype(jnp.bfloat16)
+        parts = [mm(spectrum[:, c * 256 : (c + 1) * 256], tile("far%d" % c, 0, 0)) for c in range(4)]
     with jax.named_scope("unfold"):
-        sides = [
-            jnp.concatenate([part[:, s * 128 : (s + 1) * 128] for part in parts], axis=1)
-            for s in range(2)
-        ]
-        high, low = halves(jnp.concatenate(sides, axis=0))
-        stacked = jnp.concatenate([high, low], axis=0)
-        both = mm(stacked, table("unfold", 0))
-        both = both[: 2 * n] + both[2 * n :]
-        for s, group in enumerate(groups):
-            for i, v in enumerate(group):
-                out_ref[:, v * 128 : (v + 1) * 128] = both[
-                    s * n : (s + 1) * n, i * 128 : (i + 1) * 128
-                ]
+        both = mm(unfolded(parts).astype(jnp.bfloat16), table("unfold", 0))
+        for v, value in cells_of(both):
+            at = slice(v * 128, (v + 1) * 128)
+            out_ref[:, at] = out_ref[:, at] + value
 
 
 def emit(in_ref, out_ref, sem):
@@ -766,6 +817,8 @@
     scratch += [
         pltpu.VMEM((512, 512), jnp.bfloat16),
         pltpu.VMEM((4, 256, 512), jnp.bfloat16),
+        pltpu.VMEM((2, 16, 256), jnp.bfloat16),
+        pltpu.VMEM((P_SIZE, 1024), jnp.float32),
         pltpu.VMEM((2, P_SIZE, 1024), jnp.bfloat16),
         pltpu.VMEM((2, 4 * P_SIZE, 256), jnp.bfloat16),
         pltpu.VMEM((2, 8 * P_SIZE, 256), jnp.bfloat16),

time: 13 us -> 12.8 us (0.985)
  the two profiles are of different devices: /device:TPU:0 before, /device:TPU:1 now
where the time goes in v7:
time: 12.8 us; the launch traced here: 12.7 us
  Pallas kernels  12.7 us (99%)
    pallas_call x1, Pallas kernels, body(): pl.pallas_call(functools.partial(kernel, places, n_gx, n_gy), out_shape=p...  12 us
    pallas_call x1, Pallas kernels, body(): pl.pallas_call(emit, out_shape=jax.ShapeDtypeStruct(charge.shape, charge....  0.67 us

profile of v7, /device:TPU:1, one launch (start us, length us, event | category | flops | bytes accessed | tf_op | source)
XLA Modules:
  0.0 12.7 jit_solution(7320104697761582687)
XLA Ops:
  0.0 12.0 %mlc.1.in_ref = f32[32,1024]{1,0:T(8,128)S(1)} custom-call(f32[32,1024]{1,0:T(8,128)} %refs_0_.1, f32[64,512]{1,0:T(8,128)} %constant.18.clone.refs_1_, bf16[1360,256]{1,0:T(8,128)(2,1)} %constant.19.clone.refs_2_, f32[1184,256]{1,0:T(8,128)} %constant.20.clone.refs_3_, bf16[1024,256]{1,0:T(8,128)(2,1)} %constant.21.clone.refs_4_, ...), custom_call_target="tpu_custom_call" | custom-call | tf_op jit(solution)/shard_map/mlc/pallas_call | solution.py:847
  12.0 0.7 %emit.1 = f32[32,1024]{1,0:T(8,128)} custom-call(f32[32,1024]{1,0:T(8,128)S(1)} %mlc.1.in_ref), custom_call_target="tpu_custom_call" | custom-call | tf_op jit(solution)/shard_map/emit/pallas_call | solution.py:858

commit v8 on v7

--- a/solution.py
+++ b/solution.py
@@ -340,7 +340,7 @@
     charge_ref, compact_ref, recip_ref, mine_ref, tables_ref = refs[count + 1 : count + 6]
     vmem = {"charge": charge_ref, "compact": compact_ref, "recip": recip_ref, "mine": mine_ref}
     (
-        sign_ref, grow_ref, sample_ref, spec_ref, fold_ref, w_ref, z_ref, x_ref, s_ref, b_ref, y_ref, c_ref, d_ref,
+        sign_ref, grow_ref, sample_ref, spec_ref, w_ref, z_ref, x_ref, s_ref, b_ref, y_ref, c_ref, d_ref,
         mom_ref, far_ref, near_ref, cx_ref, cy_ref, rx_ref, ry_ref, tally_ref,
         load_sem, f_send, f_recv, p_send, p_recv,
     ) = refs[count + 6 :]
@@ -422,6 +422,15 @@
 
     with jax.named_scope("w_charge"):
         loads["charge"].wait()
+        loads["compact"].wait()
+    with jax.named_scope("grow"):
+        same = lax.broadcasted_iota(jnp.int32, (16, 512), 0)
+        same = jnp.where(lax.broadcasted_iota(jnp.int32, (16, 512), 1) % 16 == same, 1.0, 0.0)
+        same = same.astype(jnp.bfloat16)
+        for t in range(4):
+            for i in range(16):
+                line = jnp.broadcast_to(compact_ref[t * 16 + i : t * 16 + i + 1], (16, 512))
+                grow_ref[t, i * 16 : (i + 1) * 16] = line.astype(jnp.bfloat16) * same
     with jax.named_scope("fold"):
         charge = vmem["charge"]
         sides = [
@@ -436,19 +445,8 @@
             for c in range(4):
                 for side in range(2):
                     piece = part[side * n : (side + 1) * n, c * 128 : (c + 1) * 128]
-                    at = c * 256 + side * 128
-                    fold_ref[k, :, at : at + 128] = piece
                     rows = (2 * k + c % 2) * n
                     w_ref[c // 2, rows : rows + n, side * 128 : (side + 1) * 128] = piece
-    with jax.named_scope("grow"):
-        loads["compact"].wait()
-        same = lax.broadcasted_iota(jnp.int32, (16, 512), 0)
-        same = jnp.where(lax.broadcasted_iota(jnp.int32, (16, 512), 1) % 16 == same, 1.0, 0.0)
-        same = same.astype(jnp.bfloat16)
-        for t in range(4):
-            for i in range(16):
-                line = jnp.broadcast_to(compact_ref[t * 16 + i : t * 16 + i + 1], (16, 512))
-                grow_ref[t, i * 16 : (i + 1) * 16] = line.astype(jnp.bfloat16) * same
     with jax.named_scope("upy"):
         for p in range(2):
             both = mm(w_ref[p], grow_ref[2 * p])
@@ -572,7 +570,7 @@
 
         return carry
 
-    early = a < n_gx // 4
+    early = a < n_gx // 8
 
     def send_far():
         with jax.named_scope("sendf"):
@@ -654,7 +652,14 @@
                 cy_ref[...] = cy
 
             with jax.named_scope("near"):
-                narrow = halves(left_mul("sn", fold_ref[0], fold_ref[1]))
+                folded = [
+                    jnp.concatenate(
+                        [w_ref[c // 2, (2 * k + c % 2) * n : (2 * k + c % 2 + 1) * n] for c in range(4)],
+                        axis=1,
+                    )
+                    for k in range(2)
+                ]
+                narrow = halves(left_mul("sn", *folded))
                 spectrum = []
                 for c in range(4):
                     at = slice(c * 256, (c + 1) * 256)
@@ -819,7 +824,6 @@
         pltpu.VMEM((4, 256, 512), jnp.bfloat16),
         pltpu.VMEM((2, 16, 256), jnp.bfloat16),
         pltpu.VMEM((P_SIZE, 1024), jnp.float32),
-        pltpu.VMEM((2, P_SIZE, 1024), jnp.bfloat16),
         pltpu.VMEM((2, 4 * P_SIZE, 256), jnp.bfloat16),
         pltpu.VMEM((2, 8 * P_SIZE, 256), jnp.bfloat16),
         pltpu.VMEM((2 * P_SIZE, 4096), jnp.bfloat16),

time: 12.8 us -> 12.7 us (level)
  the two profiles are of different devices: /device:TPU:1 before, /device:TPU:0 now
where the time goes in v8:
time: 12.7 us; the launch traced here: 12.6 us
  Pallas kernels  12.6 us (99%)
    pallas_call x1, Pallas kernels, body(): pl.pallas_call(functools.partial(kernel, places, n_gx, n_gy), out_shape=p...  11.9 us
    pallas_call x1, Pallas kernels, body(): pl.pallas_call(emit, out_shape=jax.ShapeDtypeStruct(charge.shape, charge....  0.67 us

profile of v8, /device:TPU:0, one launch (start us, length us, event | category | flops | bytes accessed | tf_op | source)
XLA Modules:
  0.0 12.6 jit_solution(8184334771414052544)
XLA Ops:
  0.0 11.9 %mlc.1.in_ref = f32[32,1024]{1,0:T(8,128)S(1)} custom-call(f32[32,1024]{1,0:T(8,128)} %refs_0_.1, f32[64,512]{1,0:T(8,128)} %constant.18.clone.refs_1_, bf16[1360,256]{1,0:T(8,128)(2,1)} %constant.19.clone.refs_2_, f32[1184,256]{1,0:T(8,128)} %constant.20.clone.refs_3_, bf16[1024,256]{1,0:T(8,128)(2,1)} %constant.21.clone.refs_4_, ...), custom_call_target="tpu_custom_call" | custom-call | tf_op jit(solution)/shard_map/mlc/pallas_call | solution.py:851
  11.9 0.7 %emit.1 = f32[32,1024]{1,0:T(8,128)} custom-call(f32[32,1024]{1,0:T(8,128)S(1)} %mlc.1.in_ref), custom_call_target="tpu_custom_call" | custom-call | tf_op jit(solution)/shard_map/emit/pallas_call | solution.py:862

commit v9 on v8

--- a/solution.py
+++ b/solution.py
@@ -314,7 +314,7 @@
     "charge", "compact", "upz", "recip", "downy", "spread", "mine", "side", "drop", "last",
 ]
 WAITS = [
-    ["charge"], ["compact"], ["upz"], ["recip"], ["downy", "spread"], ["mine"],
+    ["charge"], ["compact"], ["upz"], ["recip"], ["downy", "spread", "mine"],
     ["side", "drop", "last"],
 ]
 CUTS = {"charge": 4, "compact": 4}
@@ -372,7 +372,8 @@
                 pltpu.make_async_copy(
                     source.at[part], vmem[name].at[part], load_sem.at[i]
                 ).start()
-        target = tables_ref.at[pl.ds(start, base - start)] if base > start else vmem[names[0]]
+        extra = 2 * vmem["mine"].shape[0] * modes // 256 if "mine" in names else 0
+        target = tables_ref.at[pl.ds(start, base - start + extra)] if base > start else vmem[names[0]]
         loads[names[0]] = pltpu.make_async_copy(target, target, load_sem.at[i])
 
     barrier = pltpu.get_barrier_semaphore()
@@ -519,7 +520,6 @@
 
     def arrive():
         loads["downy"].wait()
-        loads["mine"].wait()
 
     with jax.named_scope("down"):
         y0, y1, y2, y3 = down("means", 16, b_ref, y_ref, arrive)

time: 12.7 us -> 12.7 us (level)
  no operation moved by 1% of the time
where the time goes in v9:
time: 12.7 us; the launch traced here: 12.6 us
  Pallas kernels  12.6 us (99%)
    pallas_call x1, Pallas kernels, body(): pl.pallas_call(functools.partial(kernel, places, n_gx, n_gy), out_shape=p...  11.9 us
    pallas_call x1, Pallas kernels, body(): pl.pallas_call(emit, out_shape=jax.ShapeDtypeStruct(charge.shape, charge....  0.67 us

profile of v9, /device:TPU:0, one launch (start us, length us, event | category | flops | bytes accessed | tf_op | source)
XLA Modules:
  0.0 12.6 jit_solution(15053475118160910748)
XLA Ops:
  0.0 11.9 %mlc.1.in_ref = f32[32,1024]{1,0:T(8,128)S(1)} custom-call(f32[32,1024]{1,0:T(8,128)} %refs_0_.1, f32[64,512]{1,0:T(8,128)} %constant.18.clone.refs_1_, bf16[1360,256]{1,0:T(8,128)(2,1)} %constant.19.clone.refs_2_, f32[1184,256]{1,0:T(8,128)} %constant.20.clone.refs_3_, bf16[1024,256]{1,0:T(8,128)(2,1)} %constant.21.clone.refs_4_, ...), custom_call_target="tpu_custom_call" | custom-call | tf_op jit(solution)/shard_map/mlc/pallas_call | solution.py:851
  11.9 0.7 %emit.1 = f32[32,1024]{1,0:T(8,128)} custom-call(f32[32,1024]{1,0:T(8,128)S(1)} %mlc.1.in_ref), custom_call_target="tpu_custom_call" | custom-call | tf_op jit(solution)/shard_map/emit/pallas_call | solution.py:862

commit v10 on v9

--- a/solution.py
+++ b/solution.py
@@ -450,8 +450,8 @@
                     w_ref[c // 2, rows : rows + n, side * 128 : (side + 1) * 128] = piece
     with jax.named_scope("upy"):
         for p in range(2):
-            both = mm(w_ref[p], grow_ref[2 * p])
-            lift = both[: 2 * n] + both[2 * n :] + mm(w_ref[p, 0 : 2 * n], grow_ref[2 * p + 1])
+            both = mm(w_ref[p], jnp.concatenate([grow_ref[2 * p], grow_ref[2 * p + 1]], axis=1))
+            lift = both[: 2 * n, :512] + both[2 * n :, :512] + both[: 2 * n, 512:]
             high, low = halves(lift)
             for q in range(2):
                 for k in range(4):
@@ -536,12 +536,12 @@
         packet = spread[:, :modes] + 2.0 * bend
         packet = packet - jnp.concatenate([gap, bend[:-1]]) - jnp.concatenate([bend[1:], gap])
         mine = vmem["mine"]
-        near_ref[n_gy + b] = packet
         rightward = jnp.sum(packet * mine[0:16], axis=0, keepdims=True)
         leftward = jnp.sum(packet * mine[16:32], axis=0, keepdims=True)
         for g in range(modes // 128):
             mom_ref[g, 0:1] = rightward[:, g * 128 : (g + 1) * 128]
             mom_ref[g, 1:2] = leftward[:, g * 128 : (g + 1) * 128]
+        near_ref[n_gy + b] = packet
 
     def remote(source, target, send, recv, device):
         return pltpu.make_async_remote_copy(

time: 12.7 us -> 12.7 us (level)
  no operation moved by 1% of the time
where the time goes in v10:
time: 12.7 us; the launch traced here: 12.6 us
  Pallas kernels  12.6 us (99%)
    pallas_call x1, Pallas kernels, body(): pl.pallas_call(functools.partial(kernel, places, n_gx, n_gy), out_shape=p...  11.9 us
    pallas_call x1, Pallas kernels, body(): pl.pallas_call(emit, out_shape=jax.ShapeDtypeStruct(charge.shape, charge....  0.67 us

profile of v10, /device:TPU:0, one launch (start us, length us, event | category | flops | bytes accessed | tf_op | source)
XLA Modules:
  0.0 12.6 jit_solution(827928136663360335)
XLA Ops:
  0.0 11.9 %mlc.1.in_ref = f32[32,1024]{1,0:T(8,128)S(1)} custom-call(f32[32,1024]{1,0:T(8,128)} %refs_0_.1, f32[64,512]{1,0:T(8,128)} %constant.18.clone.refs_1_, bf16[1360,256]{1,0:T(8,128)(2,1)} %constant.19.clone.refs_2_, f32[1184,256]{1,0:T(8,128)} %constant.20.clone.refs_3_, bf16[1024,256]{1,0:T(8,128)(2,1)} %constant.21.clone.refs_4_, ...), custom_call_target="tpu_custom_call" | custom-call | tf_op jit(solution)/shard_map/mlc/pallas_call | solution.py:851
  11.9 0.7 %emit.1 = f32[32,1024]{1,0:T(8,128)} custom-call(f32[32,1024]{1,0:T(8,128)S(1)} %mlc.1.in_ref), custom_call_target="tpu_custom_call" | custom-call | tf_op jit(solution)/shard_map/emit/pallas_call | solution.py:862
